TPU v7x, 128 devices: a whole 4x4x4 slice. The times are simulated.
128 devices in a mesh: gx: 4 (over y), gy: 32 (over x, z, core).
Axes of the slice: x: 4, y: 4, z: 4, core: 2. Of those that a mesh axis runs over, the one named last changes fastest.
Arguments:
- fluid_state: float32 [4, 32, 256, 512], P(None, None, 'gy', 'gx'), may hold values from -6 to 6
- particle_pos: float32 [3, 1048576], P(None, ('gx', 'gy')), may hold values from -6 to 6
- particle_motion: float32 [6, 1048576], P(None, ('gx', 'gy')), may hold values from -6 to 6
- particle_radius: float32 [1048576], P(('gx', 'gy')), may hold values from 0.5 to 1
- particle_temp: float32 [1048576], P(('gx', 'gy')), may hold values from -6 to 6
- particle_cell: int32 [1048576], P(('gx', 'gy')), may hold values from 0 to 32767
- particle_box: int32 [1048576, 1], P(('gx', 'gy')), may hold values from 0 to 127; in each aligned block of 8192 rows (0 to 8191, 8192 to 16383, ...) at most 128 rows name the same one
- box_owner: int32 [128], replicated, may hold values from 0 to 127, each once
- contact_mask: int32 [16384, 128, 128], P(('gx', 'gy')), may hold values 0 or 1
Outputs:
- fluid_next: float32 [4, 32, 256, 512], P(None, None, 'gy', 'gx')
- void_fraction: float32 [32, 256, 512], P(None, 'gy', 'gx')
- particle_next: float32 [7, 1048576], P(None, ('gx', 'gy'))
Inputs may be any that keep to these rules, and one draw needn't show every extreme that they name: `particle_box`: among the 8192 rows of one device no box is named by more than 128 rows, a bound that some block reaches. `box_owner`: A permutation of the devices.
All inputs are finite; a program needn't handle non-finite values. No bound on the sum of `contact_mask` on one device may be relied on, other than what follows from the above.
Results may differ from a plain program's by a relative error of at most 0.0003.
Values sent between devices are 32-bit elements; how exact they have to be, the bound alone decides.
A program may use at most 64 MiB of HBM per device.

v0:
```python
import jax
import jax.numpy as jnp
from jax import lax
from jax.sharding import Mesh
from jax.sharding import PartitionSpec as P

GX_GY = ("gx", "gy_0", "gy_1", "gy_2")
GY = ("gy_0", "gy_1", "gy_2")


TIME_STEP = 0.1
STIFFNESS = 0.5
DAMPING_RATE = 0.2
ROTATION_DRAG = 0.1
DRAG_COEFF = 4.0
CONDUCTION = 0.3
HEAT_TRANSFER = 4.0
GRAVITY = 0.3
COUPLING = 4.0
CENTRE_WEIGHT = 0.25
SIDE_WEIGHT = 0.125


def with_halo(value, sides, width):
    edges = {}
    for axis, dim in sides:
        size, length = (lax.axis_size(axis), value.shape[dim])
        up = [(i, (i + 1) % size) for i in range(size - 1)]
        last = lax.slice_in_dim(value, length - width, length, axis=dim)
        first = lax.slice_in_dim(value, 0, width, axis=dim)
        edges[dim] = (
            lax.ppermute(last, axis, up),
            lax.ppermute(first, axis, [(b, a) for a, b in up]),
        )
    done = []
    for _, dim in sides:
        low, high = edges[dim]
        around = [(width, width) if d in done else (0, 0) for d in range(value.ndim)]
        value = jnp.concatenate([jnp.pad(low, around), value, jnp.pad(high, around)], axis=dim)
        done.append(dim)
    return value


def cut_along(value, dim, size):
    lengths = value.shape
    pieces = value.reshape(*lengths[:dim], size, lengths[dim] // size, *lengths[dim + 1 :])
    return jnp.moveaxis(pieces, dim, 0)


def in_order(pieces, dim):
    lengths = list(pieces.shape[1:])
    lengths[dim] *= pieces.shape[0]
    return jnp.moveaxis(pieces, 0, dim).reshape(lengths)


def turned_blocks(pieces, axes, order):
    lengths = [lax.axis_size(a) for a in axes]
    pieces = pieces.reshape(*lengths, *pieces.shape[1:])
    for k in order:
        pieces = lax.all_to_all(pieces, axes[k], split_axis=k, concat_axis=k, tiled=True)
    return pieces.reshape(-1, *pieces.shape[len(axes) :])


def exchange_by_chip(value, groups, order, split_dim, concat_dim):
    size = lax.axis_size(groups[0]) * lax.axis_size(groups[1])
    pieces = cut_along(value, split_dim, size)
    return in_order(turned_blocks(pieces, groups, order), concat_dim)


def stencil(padded):
    interior = padded[:, :, 1:-1, 1:-1]
    z_padded = jnp.pad(interior, ((0, 0), (1, 1), (0, 0), (0, 0)))
    beside_all = z_padded[:, 2:] + z_padded[:, :-2]
    beside_all = beside_all + padded[:, :, 2:, 1:-1] + padded[:, :, :-2, 1:-1]
    beside_all = beside_all + padded[:, :, 1:-1, 2:] + padded[:, :, 1:-1, :-2]
    return CENTRE_WEIGHT * interior + SIDE_WEIGHT * beside_all


def one_hot(indices, count, dtype):
    return (indices[:, None] == jnp.arange(count, dtype=jnp.int32)[None, :]).astype(dtype)


def contact(arrived, mask_blocks):
    position = arrived[0:3]
    velocity = arrived[3:6]
    angular = arrived[6:9]
    fluid_vel = arrived[9:12]
    radius = arrived[12]
    solid_temp = arrived[13]
    gas_temp = arrived[14]
    occupied = (radius > 0.0).astype(jnp.float32)
    pair_mask = mask_blocks.astype(jnp.float32) * occupied[:, :, None] * occupied[:, None, :]
    distance = jnp.zeros(pair_mask.shape, jnp.float32)
    for component in range(3):
        offset = position[component][:, :, None] - position[component][:, None, :]
        distance = distance + offset * offset
    reach_sq = (radius[:, :, None] + radius[:, None, :]) ** 2 + 1.0
    weight = pair_mask * jnp.exp(-distance / reach_sq)
    weight_sum = jnp.sum(weight, axis=2)
    stacked = jnp.concatenate([position, velocity, angular, solid_temp[None]], axis=0)
    mixed = jnp.einsum("bij,cbj->cbi", weight, stacked, precision=lax.Precision.HIGHEST)
    spring = position * weight_sum - mixed[0:3]
    damping = velocity * weight_sum - mixed[3:6]
    drag_force = DRAG_COEFF / (radius * radius + 0.25) * (fluid_vel - velocity)
    upward = jnp.array([0.0, 0.0, 1.0], jnp.float32)[:, None, None]
    velocity_next = (
        velocity
        + TIME_STEP * (STIFFNESS * spring - DAMPING_RATE * damping + drag_force)
        - TIME_STEP * GRAVITY * upward
    )
    angular_next = angular - TIME_STEP * ROTATION_DRAG * (angular * weight_sum + mixed[6:9])
    temp_next = solid_temp + TIME_STEP * (
        CONDUCTION * (mixed[9] - solid_temp * weight_sum) + HEAT_TRANSFER * (gas_temp - solid_temp)
    )
    return jnp.concatenate([velocity_next, angular_next, drag_force, temp_next[None]], axis=0)


def shards(
    fluid_state,
    particle_pos,
    particle_motion,
    particle_radius,
    particle_temp,
    particle_cell,
    particle_box,
    box_owner,
    contact_mask,
):
    devices = lax.axis_size(GX_GY)
    particles = particle_pos.shape[1]
    peer_slots = 2 * particles // devices
    grid_layers = fluid_state.shape[1]
    grid_rows = fluid_state.shape[2]
    grid_cols = fluid_state.shape[3]
    plane_rows = grid_layers * grid_rows
    block_rows = min(particles, 1024)
    num_blocks = particles // block_rows
    highest = lax.Precision.HIGHEST
    padded = with_halo(fluid_state, (("gx", 3), (GY, 2)), 1)
    filtered = stencil(padded).reshape(4, plane_rows, grid_cols)
    cell_high = (particle_cell // grid_cols).reshape(num_blocks, block_rows)
    cell_low = (particle_cell % grid_cols).reshape(num_blocks, block_rows)

    def look_up(pieces):
        high_ids, low_ids = pieces
        partial_rows = jnp.einsum(
            "khl,pl->kph", filtered, one_hot(low_ids, grid_cols, jnp.float32), precision=highest
        )
        return jnp.sum(partial_rows * one_hot(high_ids, plane_rows, jnp.float32)[None], axis=2)

    at_particle = lax.map(look_up, (cell_high, cell_low)).transpose(1, 0, 2).reshape(4, particles)
    box_ids = particle_box[:, 0]
    device_ids = jnp.arange(devices, dtype=jnp.int32)
    box_match = box_ids[:, None] == device_ids[None, :]
    owner_dev = jnp.sum(jnp.where(box_match, box_owner[None, :], 0), axis=1)
    owner_hot = one_hot(owner_dev, devices, jnp.bfloat16).reshape(num_blocks, block_rows, devices)
    positions = jnp.arange(block_rows, dtype=jnp.int32)
    lower = (positions[:, None] > positions[None, :]).astype(jnp.bfloat16)
    within = jnp.einsum("ij,bjo->bio", lower, owner_hot, preferred_element_type=jnp.float32)
    block_counts = jnp.sum(owner_hot.astype(jnp.float32), axis=1)
    before = jnp.cumsum(block_counts, axis=0) - block_counts
    slot_rank = jnp.sum(
        (within + before[:, None, :]) * owner_hot.astype(jnp.float32), axis=2
    ).astype(jnp.int32)
    owner_blocks = owner_dev.reshape(num_blocks, block_rows)
    payload = jnp.concatenate(
        [
            particle_pos,
            particle_motion,
            at_particle[0:3],
            particle_radius[None],
            particle_temp[None],
            at_particle[3:4],
        ],
        axis=0,
    )
    payload_blocks = payload.reshape(15, num_blocks, block_rows).transpose(1, 0, 2)

    def place(total, pieces):
        values, owners, ranks = pieces
        weighted = values[:, :, None] * one_hot(owners, devices, jnp.float32)[None]
        added = jnp.einsum(
            "cpo,pr->cor", weighted, one_hot(ranks, peer_slots, jnp.float32), precision=highest
        )
        return (total + added, None)

    outgoing, _ = lax.scan(
        place,
        jnp.zeros((15, devices, peer_slots), jnp.float32),
        (payload_blocks, owner_blocks, slot_rank),
    )
    arrived = exchange_by_chip(outgoing, (("gx", "gy_0", "gy_1"), "gy_2"), (0, 1), 1, 1)
    result = contact(arrived, contact_mask)
    returned = lax.all_to_all(result, GX_GY, split_axis=1, concat_axis=1, tiled=True)

    def fetch(pieces):
        owners, ranks = pieces
        partial_rows = jnp.einsum(
            "cor,pr->cpo", returned, one_hot(ranks, peer_slots, jnp.float32), precision=highest
        )
        return jnp.sum(partial_rows * one_hot(owners, devices, jnp.float32)[None], axis=2)

    back = lax.map(fetch, (owner_blocks, slot_rank)).transpose(1, 0, 2).reshape(10, particles)
    particle_next = jnp.concatenate([back[0:6], back[9:10]], axis=0)
    volume = particle_radius**3
    deposit_terms = jnp.concatenate(
        [volume[None], -volume[None] * back[6:9], (volume * (back[9] - at_particle[3]))[None]],
        axis=0,
    )
    term_blocks = deposit_terms.reshape(5, num_blocks, block_rows).transpose(1, 0, 2)

    def deposit(total, pieces):
        values, high_ids, low_ids = pieces
        weighted = values[:, :, None] * one_hot(high_ids, plane_rows, jnp.float32)[None]
        added = jnp.einsum(
            "kph,pl->khl", weighted, one_hot(low_ids, grid_cols, jnp.float32), precision=highest
        )
        return (total + added, None)

    deposits, _ = lax.scan(
        deposit,
        jnp.zeros((5, plane_rows, grid_cols), jnp.float32),
        (term_blocks, cell_high, cell_low),
    )
    deposits = deposits.reshape(5, grid_layers, grid_rows, grid_cols)
    deposit_pad = with_halo(deposits, (("gx", 3), (GY, 2)), 1)
    spread = stencil(deposit_pad)
    crowding = 1.0 + COUPLING * spread[0]
    void_fraction = 1.0 / crowding
    fluid_next = jnp.concatenate(
        [
            fluid_state[0:3] + TIME_STEP * COUPLING * spread[1:4] * crowding,
            fluid_state[3:4] + TIME_STEP * COUPLING * spread[4:5] * crowding,
        ],
        axis=0,
    )
    return (fluid_next, void_fraction, particle_next)


def solution(mesh):
    split = Mesh(mesh.devices.reshape(mesh.shape["gx"], 4, 4, 2), ("gx", "gy_0", "gy_1", "gy_2"))
    return jax.shard_map(
        shards,
        mesh=split,
        in_specs=(
            P(None, None, GY, "gx"),
            P(None, GX_GY),
            P(None, GX_GY),
            P(GX_GY),
            P(GX_GY),
            P(GX_GY),
            P(GX_GY, None),
            P(),
            P(GX_GY, None, None),
        ),
        out_specs=(P(None, None, GY, "gx"), P(None, GY, "gx"), P(None, GX_GY)),
        check_vma=False,
    )
```

profile of v0, /device:TPU:10, one launch (start us, length us, event | category | flops | bytes accessed | tf_op | source)
XLA Modules:
  0.0 238.9 jit_solution(7609871436315913729)
XLA Ops:
  0.6 2.2 fusion.90
  2.8 3.6 %collective-permute-start = (f32[4,32,8,1]{3,2,1,0:T(8,128)}, f32[4,32,8,1]{3,2,1,0:T(8,128)S(1)}, u32[]{:S(2)}, u32[]{:S(2)}) collective-permute-start(f32[4,32,8,1]{3,2,1,0:T(8,128)} %get-tuple-element.247), channel_id=1, source_target_pairs={{0,32},{32,64},{64,96},{1,33},{33,65},{65,97},{2,34},{34,66},{66,9... | collective-permute-start | bytes 12296 | tf_op jit(solution)/shard_map/ppermute | solution.py:32
  6.5 2.4 collective-permute-start.1
  10.8 4.8 %collective-permute-start.2 = (f32[4,32,1,128]{3,2,1,0:T(1,128)}, f32[4,32,1,128]{3,2,1,0:T(1,128)S(1)}, u32[]{:S(2)}, u32[]{:S(2)}) collective-permute-start(f32[4,32,1,128]{3,2,1,0:T(1,128)} %get-tuple-element.244), channel_id=1, source_target_pairs={{1,0},{2,1},{3,2},{4,3},{5,4},{6,5},{7,6},{8,7},{9,8},{10,9},{11,1... | collective-permute-start | bytes 196616 | tf_op jit(solution)/shard_map/ppermute | solution.py:33
  17.5 3.3 %select_reduce_fusion = s32[8192]{0:T(1024)S(1)} fusion(s32[128]{0:T(128)} %param.25, s32[8192]{0:T(1024)} %bitcast.202), kind=kLoop, calls=%fused_computation.52 | loop fusion | flops 3137536 | bytes 66048 | tf_op jit(solution)/shard_map/reduce_sum | solution.py:155
  21.4 3.3 %fusion.30 = f32[8,1024]{1,0:T(8,128)} fusion(f32[8,128]{1,0:T(8,128)S(1)} %sub.101, s32[8,1024]{1,0:T(8,128)S(1)} %reshape.284), kind=kOutput, calls=%fused_computation.47 | convolution fusion | flops 2155864064 | bytes 69632 | tf_op jit(solution)/shard_map/ij,bjo->bio/dot_general | solution.py:159
  26.4 18.9 %while.42 = (s32[]{:T(128)}, f32[8,4,1024]{2,1,0:T(4,128)S(1)}, s32[8,1024]{1,0:T(8,128)S(1)}, f32[4,256,128]{2,1,0:T(8,128)S(1)}, s32[8,1024]{1,0:T(8,128)S(1)}, /*index=5*/s32[]{:T(128)}) while((s32[]{:T(128)}, f32[8,4,1024]{2,1,0:T(4,128)S(1)}, s32[8,1024]{1,0:T(8,128)S(1)}, f32[4,256,128]{2,1,0:T(8,128)S(1)}, s32[8,1024]{1,0:T(8,128)S(1)}, ...), condition=%wide.region_6.7_spmd, body=%wide.region_4.6_spmd.sunk | while | flops 1613361152 | bytes 2695245 | solution.py:151
  26.5 2.2 multiply_reduce_fusion.4
  28.9 2.2 multiply_reduce_fusion.4
  33.6 2.2 multiply_reduce_fusion.4
  38.4 2.2 multiply_reduce_fusion.4
  43.1 2.2 multiply_reduce_fusion.4
  46.0 37.5 %while.44 = (s32[]{:T(128)}, f32[15,128,128]{2,1,0:T(8,128)S(1)}, f32[8,15,1024]{2,1,0:T(8,128)S(1)}, s32[8,1024]{1,0:T(8,128)S(1)}, s32[8,1024]{1,0:T(8,128)S(1)}, /*index=5*/s32[]{:T(128)}, s32[]{:T(128)}) while((s32[]{:T(128)}, f32[15,128,128]{2,1,0:T(8,128)S(1)}, f32[8,15,1024]{2,1,0:T(8,128)S(1)}, s32[8,1024]{1,0:T(8,128)S(1)}, ...), condition=%wide.region_8.9_spmd.clone, body=%wide.region_7.8_spmd.clone.sunk | while | flops 3022749696 | bytes 3223647 | solution.py:187
  46.2 4.5 %fusion.117 = f32[15,128,128]{2,1,0:T(8,128)S(1)} fusion(f32[1024,128]{0,1:T(8,128)S(1)} %fusion.116, f32[15,1024]{1,0:T(8,128)S(1)} %dynamic-slice_bitcast_fusion.4, f32[15,128,128]{2,1,0:T(8,128)S(1)} %get-tuple-element.419, pred[]{:T(512)S(6)} %compare.31, s32[1024]{0:T(1024)S(1)} %bitcast.197), kind=kOutput, calls=%fused_computation.22.clone.1 | convolution fusion | flops 3022487552 | bytes 2555905 | tf_op jit(solution)/shard_map/while/body/eval_jaxpr/cpo,pr->cor/dot_general | solution.py:182
  50.8 4.5 %fusion.117 = f32[15,128,128]{2,1,0:T(8,128)S(1)} fusion(f32[1024,128]{0,1:T(8,128)S(1)} %fusion.116, f32[15,1024]{1,0:T(8,128)S(1)} %dynamic-slice_bitcast_fusion.4, f32[15,128,128]{2,1,0:T(8,128)S(1)} %get-tuple-element.419, pred[]{:T(512)S(6)} %compare.31, s32[1024]{0:T(1024)S(1)} %bitcast.197), kind=kOutput, calls=%fused_computation.22.clone.1 | convolution fusion | flops 3022487552 | bytes 2555905 | tf_op jit(solution)/shard_map/while/body/eval_jaxpr/cpo,pr->cor/dot_general | solution.py:182
  55.5 4.5 %fusion.117 = f32[15,128,128]{2,1,0:T(8,128)S(1)} fusion(f32[1024,128]{0,1:T(8,128)S(1)} %fusion.116, f32[15,1024]{1,0:T(8,128)S(1)} %dynamic-slice_bitcast_fusion.4, f32[15,128,128]{2,1,0:T(8,128)S(1)} %get-tuple-element.419, pred[]{:T(512)S(6)} %compare.31, s32[1024]{0:T(1024)S(1)} %bitcast.197), kind=kOutput, calls=%fused_computation.22.clone.1 | convolution fusion | flops 3022487552 | bytes 2555905 | tf_op jit(solution)/shard_map/while/body/eval_jaxpr/cpo,pr->cor/dot_general | solution.py:182
  60.1 4.5 %fusion.117 = f32[15,128,128]{2,1,0:T(8,128)S(1)} fusion(f32[1024,128]{0,1:T(8,128)S(1)} %fusion.116, f32[15,1024]{1,0:T(8,128)S(1)} %dynamic-slice_bitcast_fusion.4, f32[15,128,128]{2,1,0:T(8,128)S(1)} %get-tuple-element.419, pred[]{:T(512)S(6)} %compare.31, s32[1024]{0:T(1024)S(1)} %bitcast.197), kind=kOutput, calls=%fused_computation.22.clone.1 | convolution fusion | flops 3022487552 | bytes 2555905 | tf_op jit(solution)/shard_map/while/body/eval_jaxpr/cpo,pr->cor/dot_general | solution.py:182
  64.8 4.5 %fusion.117 = f32[15,128,128]{2,1,0:T(8,128)S(1)} fusion(f32[1024,128]{0,1:T(8,128)S(1)} %fusion.116, f32[15,1024]{1,0:T(8,128)S(1)} %dynamic-slice_bitcast_fusion.4, f32[15,128,128]{2,1,0:T(8,128)S(1)} %get-tuple-element.419, pred[]{:T(512)S(6)} %compare.31, s32[1024]{0:T(1024)S(1)} %bitcast.197), kind=kOutput, calls=%fused_computation.22.clone.1 | convolution fusion | flops 3022487552 | bytes 2555905 | tf_op jit(solution)/shard_map/while/body/eval_jaxpr/cpo,pr->cor/dot_general | solution.py:182
  69.5 4.5 %fusion.117 = f32[15,128,128]{2,1,0:T(8,128)S(1)} fusion(f32[1024,128]{0,1:T(8,128)S(1)} %fusion.116, f32[15,1024]{1,0:T(8,128)S(1)} %dynamic-slice_bitcast_fusion.4, f32[15,128,128]{2,1,0:T(8,128)S(1)} %get-tuple-element.419, pred[]{:T(512)S(6)} %compare.31, s32[1024]{0:T(1024)S(1)} %bitcast.197), kind=kOutput, calls=%fused_computation.22.clone.1 | convolution fusion | flops 3022487552 | bytes 2555905 | tf_op jit(solution)/shard_map/while/body/eval_jaxpr/cpo,pr->cor/dot_general | solution.py:182
  74.1 4.5 %fusion.117 = f32[15,128,128]{2,1,0:T(8,128)S(1)} fusion(f32[1024,128]{0,1:T(8,128)S(1)} %fusion.116, f32[15,1024]{1,0:T(8,128)S(1)} %dynamic-slice_bitcast_fusion.4, f32[15,128,128]{2,1,0:T(8,128)S(1)} %get-tuple-element.419, pred[]{:T(512)S(6)} %compare.31, s32[1024]{0:T(1024)S(1)} %bitcast.197), kind=kOutput, calls=%fused_computation.22.clone.1 | convolution fusion | flops 3022487552 | bytes 2555905 | tf_op jit(solution)/shard_map/while/body/eval_jaxpr/cpo,pr->cor/dot_general | solution.py:182
  78.8 4.5 %fusion.117 = f32[15,128,128]{2,1,0:T(8,128)S(1)} fusion(f32[1024,128]{0,1:T(8,128)S(1)} %fusion.116, f32[15,1024]{1,0:T(8,128)S(1)} %dynamic-slice_bitcast_fusion.4, f32[15,128,128]{2,1,0:T(8,128)S(1)} %get-tuple-element.419, pred[]{:T(512)S(6)} %compare.31, s32[1024]{0:T(1024)S(1)} %bitcast.197), kind=kOutput, calls=%fused_computation.22.clone.1 | convolution fusion | flops 3022487552 | bytes 2555905 | tf_op jit(solution)/shard_map/while/body/eval_jaxpr/cpo,pr->cor/dot_general | solution.py:182
  83.9 23.5 %all_to_all.15 = f32[64,2,15,1,128]{4,1,2,3,0:T(2,128)S(1)} all-to-all(f32[64,2,15,1,128]{4,1,2,3,0:T(2,128)S(1)} %copy.83), channel_id=1, replica_groups=mesh['gx'=4,'gy_0'=4,'gy_1'=4,'gy_2'=2] {'gx','gy_0','gy_1'}, dimensions={0} | all-to-all | bytes 1966080 | tf_op jit(solution)/shard_map/all_to_all | solution.py:60
  107.5 5.3 %all_to_all.16 = f32[64,2,15,1,128]{4,0,2,3,1:T(8,128)S(1)} all-to-all(f32[64,2,15,1,128]{4,0,2,3,1:T(8,128)S(1)} %copy.84), channel_id=1, replica_groups=mesh['gx'=4,'gy_0'=4,'gy_1'=4,'gy_2'=2] {'gy_2'}, dimensions={1} | all-to-all | bytes 1966080 | tf_op jit(solution)/shard_map/all_to_all | solution.py:60
  113.7 16.1 %fusion.85 = (f32[128,128]{1,0:T(8,128)S(1)}, f32[128,128,128]{2,1,0:T(8,128)S(1)}) fusion(f32[128,128]{1,0:T(8,128)S(1)} %get-tuple-element.234, f32[128,128]{1,0:T(8,128)S(1)} %get-tuple-element.231, f32[128,128]{1,0:T(8,128)S(1)} %get-tuple-element.232, f32[128,128]{1,0:T(8,128)S(1)} %get-tuple-element.233, f32[128,128]{1,0:T(8,128)S(1)} %compare_convert_fusion, ...), kind=kLoop, calls=%fused_computation.163 | loop fusion | flops 37732352 | bytes 17170432 | tf_op jit(solution)/shard_map/reduce_sum | solution.py:99
  129.8 13.3 %fusion.38 = f32[128,10,128]{2,1,0:T(8,128)S(1)} fusion(f32[128,128,128]{2,1,0:T(8,128)S(1)} %get-tuple-element.217, f32[10,128,128]{2,1,0:T(8,128)S(1)} %pad_maximum_fusion.6), kind=kOutput, calls=%fused_computation.56 | convolution fusion | flops 251658240 | bytes 9699328 | tf_op jit(solution)/shard_map/bij,cbj->cbi/dot_general | solution.py:101
  145.0 7.4 %all-to-all-start.2 = ((f32[10,128,128]{2,0,1:T(8,128)}), f32[10,128,128]{2,0,1:T(8,128)S(1)}, u32[]{:S(2)}, u32[]{:S(2)}) async-start(f32[10,128,128]{2,0,1:T(8,128)} %copy.88), calls=%async_computation.2 | async-start | bytes 2097152 | tf_op jit(solution)/shard_map/all_to_all | solution.py:194
  152.5 18.2 %all-to-all-done.2 = f32[10,128,128]{2,0,1:T(8,128)S(1)} async-done(((f32[10,128,128]{2,0,1:T(8,128)}), f32[10,128,128]{2,0,1:T(8,128)S(1)}, u32[]{:S(2)}, u32[]{:S(2)}) %all-to-all-start.2) | async-done | bytes 655392 | tf_op jit(solution)/shard_map/all_to_all | solution.py:194
  170.9 21.6 %while.43 = (s32[]{:T(128)}, f32[8,10,1024]{2,1,0:T(8,128)S(1)}, s32[8,1024]{1,0:T(8,128)S(1)}, f32[10,128,128]{2,1,0:T(8,128)S(1)}, s32[8,1024]{1,0:T(8,128)S(1)}, /*index=5*/s32[]{:T(128)}) while((s32[]{:T(128)}, f32[8,10,1024]{2,1,0:T(8,128)S(1)}, s32[8,1024]{1,0:T(8,128)S(1)}, f32[10,128,128]{2,1,0:T(8,128)S(1)}, ...), condition=%wide.region_12.13_spmd, body=%wide.region_10.12_spmd.sunk | while | flops 2016270336 | bytes 1900621 | solution.py:203
  171.0 2.6 %multiply_reduce_fusion.5 = f32[1024,10]{0,1:T(8,128)S(1)} fusion(f32[1024,128]{0,1:T(8,128)S(1)} %fusion.113, f32[10,128,128]{2,1,0:T(8,128)S(1)} %get-tuple-element.447, s32[1024]{0:T(1024)S(1)} %bitcast.200), kind=kOutput, calls=%fused_computation.9.clone.1 | convolution fusion | flops 2016008192 | bytes 1224704 | tf_op jit(solution)/shard_map/while/body/eval_jaxpr/cor,pr->cpo/dot_general | solution.py:198
  173.7 2.6 %multiply_reduce_fusion.5 = f32[1024,10]{0,1:T(8,128)S(1)} fusion(f32[1024,128]{0,1:T(8,128)S(1)} %fusion.113, f32[10,128,128]{2,1,0:T(8,128)S(1)} %get-tuple-element.447, s32[1024]{0:T(1024)S(1)} %bitcast.200), kind=kOutput, calls=%fused_computation.9.clone.1 | convolution fusion | flops 2016008192 | bytes 1224704 | tf_op jit(solution)/shard_map/while/body/eval_jaxpr/cor,pr->cpo/dot_general | solution.py:198
  176.4 2.6 %multiply_reduce_fusion.5 = f32[1024,10]{0,1:T(8,128)S(1)} fusion(f32[1024,128]{0,1:T(8,128)S(1)} %fusion.113, f32[10,128,128]{2,1,0:T(8,128)S(1)} %get-tuple-element.447, s32[1024]{0:T(1024)S(1)} %bitcast.200), kind=kOutput, calls=%fused_computation.9.clone.1 | convolution fusion | flops 2016008192 | bytes 1224704 | tf_op jit(solution)/shard_map/while/body/eval_jaxpr/cor,pr->cpo/dot_general | solution.py:198
  179.1 2.6 %multiply_reduce_fusion.5 = f32[1024,10]{0,1:T(8,128)S(1)} fusion(f32[1024,128]{0,1:T(8,128)S(1)} %fusion.113, f32[10,128,128]{2,1,0:T(8,128)S(1)} %get-tuple-element.447, s32[1024]{0:T(1024)S(1)} %bitcast.200), kind=kOutput, calls=%fused_computation.9.clone.1 | convolution fusion | flops 2016008192 | bytes 1224704 | tf_op jit(solution)/shard_map/while/body/eval_jaxpr/cor,pr->cpo/dot_general | solution.py:198
  181.8 2.6 %multiply_reduce_fusion.5 = f32[1024,10]{0,1:T(8,128)S(1)} fusion(f32[1024,128]{0,1:T(8,128)S(1)} %fusion.113, f32[10,128,128]{2,1,0:T(8,128)S(1)} %get-tuple-element.447, s32[1024]{0:T(1024)S(1)} %bitcast.200), kind=kOutput, calls=%fused_computation.9.clone.1 | convolution fusion | flops 2016008192 | bytes 1224704 | tf_op jit(solution)/shard_map/while/body/eval_jaxpr/cor,pr->cpo/dot_general | solution.py:198
  184.5 2.6 %multiply_reduce_fusion.5 = f32[1024,10]{0,1:T(8,128)S(1)} fusion(f32[1024,128]{0,1:T(8,128)S(1)} %fusion.113, f32[10,128,128]{2,1,0:T(8,128)S(1)} %get-tuple-element.447, s32[1024]{0:T(1024)S(1)} %bitcast.200), kind=kOutput, calls=%fused_computation.9.clone.1 | convolution fusion | flops 2016008192 | bytes 1224704 | tf_op jit(solution)/shard_map/while/body/eval_jaxpr/cor,pr->cpo/dot_general | solution.py:198
  187.2 2.6 %multiply_reduce_fusion.5 = f32[1024,10]{0,1:T(8,128)S(1)} fusion(f32[1024,128]{0,1:T(8,128)S(1)} %fusion.113, f32[10,128,128]{2,1,0:T(8,128)S(1)} %get-tuple-element.447, s32[1024]{0:T(1024)S(1)} %bitcast.200), kind=kOutput, calls=%fused_computation.9.clone.1 | convolution fusion | flops 2016008192 | bytes 1224704 | tf_op jit(solution)/shard_map/while/body/eval_jaxpr/cor,pr->cpo/dot_general | solution.py:198
  189.9 2.6 %multiply_reduce_fusion.5 = f32[1024,10]{0,1:T(8,128)S(1)} fusion(f32[1024,128]{0,1:T(8,128)S(1)} %fusion.113, f32[10,128,128]{2,1,0:T(8,128)S(1)} %get-tuple-element.447, s32[1024]{0:T(1024)S(1)} %bitcast.200), kind=kOutput, calls=%fused_computation.9.clone.1 | convolution fusion | flops 2016008192 | bytes 1224704 | tf_op jit(solution)/shard_map/while/body/eval_jaxpr/cor,pr->cpo/dot_general | solution.py:198
  193.7 26.1 %while.45 = (s32[]{:T(128)}, f32[5,256,128]{2,1,0:T(8,128)S(1)}, f32[8,5,1024]{2,1,0:T(8,128)S(1)}, s32[8,1024]{1,0:T(8,128)S(1)}, s32[8,1024]{1,0:T(8,128)S(1)}, /*index=5*/s32[]{:T(128)}, s32[]{:T(128)}) while((s32[]{:T(128)}, f32[5,256,128]{2,1,0:T(8,128)S(1)}, f32[8,5,1024]{2,1,0:T(8,128)S(1)}, s32[8,1024]{1,0:T(8,128)S(1)}, ...), condition=%wide.region_14.15_spmd.clone, body=%wide.region_13.14_spmd.clone.sunk | while | flops 2015559680 | bytes 3493983 | solution.py:220
  193.9 3.1 %fusion.121 = f32[5,256,128]{2,1,0:T(8,128)S(1)} fusion(f32[1024,256]{0,1:T(8,128)S(1)} %fusion.120, f32[5,1024]{1,0:T(8,128)S(1)} %dynamic-slice_bitcast_fusion.5, f32[5,256,128]{2,1,0:T(8,128)S(1)} %get-tuple-element.458, pred[]{:T(512)S(6)} %compare.32, s32[1024]{0:T(1024)S(1)} %bitcast.198), kind=kOutput, calls=%fused_computation.35.clone.1 | convolution fusion | flops 2015035392 | bytes 2383873 | tf_op jit(solution)/shard_map/while/body/eval_jaxpr/kph,pl->khl/dot_general | solution.py:215
  197.1 3.1 %fusion.121 = f32[5,256,128]{2,1,0:T(8,128)S(1)} fusion(f32[1024,256]{0,1:T(8,128)S(1)} %fusion.120, f32[5,1024]{1,0:T(8,128)S(1)} %dynamic-slice_bitcast_fusion.5, f32[5,256,128]{2,1,0:T(8,128)S(1)} %get-tuple-element.458, pred[]{:T(512)S(6)} %compare.32, s32[1024]{0:T(1024)S(1)} %bitcast.198), kind=kOutput, calls=%fused_computation.35.clone.1 | convolution fusion | flops 2015035392 | bytes 2383873 | tf_op jit(solution)/shard_map/while/body/eval_jaxpr/kph,pl->khl/dot_general | solution.py:215
  200.4 3.1 %fusion.121 = f32[5,256,128]{2,1,0:T(8,128)S(1)} fusion(f32[1024,256]{0,1:T(8,128)S(1)} %fusion.120, f32[5,1024]{1,0:T(8,128)S(1)} %dynamic-slice_bitcast_fusion.5, f32[5,256,128]{2,1,0:T(8,128)S(1)} %get-tuple-element.458, pred[]{:T(512)S(6)} %compare.32, s32[1024]{0:T(1024)S(1)} %bitcast.198), kind=kOutput, calls=%fused_computation.35.clone.1 | convolution fusion | flops 2015035392 | bytes 2383873 | tf_op jit(solution)/shard_map/while/body/eval_jaxpr/kph,pl->khl/dot_general | solution.py:215
  203.7 3.1 %fusion.121 = f32[5,256,128]{2,1,0:T(8,128)S(1)} fusion(f32[1024,256]{0,1:T(8,128)S(1)} %fusion.120, f32[5,1024]{1,0:T(8,128)S(1)} %dynamic-slice_bitcast_fusion.5, f32[5,256,128]{2,1,0:T(8,128)S(1)} %get-tuple-element.458, pred[]{:T(512)S(6)} %compare.32, s32[1024]{0:T(1024)S(1)} %bitcast.198), kind=kOutput, calls=%fused_computation.35.clone.1 | convolution fusion | flops 2015035392 | bytes 2383873 | tf_op jit(solution)/shard_map/while/body/eval_jaxpr/kph,pl->khl/dot_general | solution.py:215
  206.9 3.1 %fusion.121 = f32[5,256,128]{2,1,0:T(8,128)S(1)} fusion(f32[1024,256]{0,1:T(8,128)S(1)} %fusion.120, f32[5,1024]{1,0:T(8,128)S(1)} %dynamic-slice_bitcast_fusion.5, f32[5,256,128]{2,1,0:T(8,128)S(1)} %get-tuple-element.458, pred[]{:T(512)S(6)} %compare.32, s32[1024]{0:T(1024)S(1)} %bitcast.198), kind=kOutput, calls=%fused_computation.35.clone.1 | convolution fusion | flops 2015035392 | bytes 2383873 | tf_op jit(solution)/shard_map/while/body/eval_jaxpr/kph,pl->khl/dot_general | solution.py:215
  210.2 3.1 %fusion.121 = f32[5,256,128]{2,1,0:T(8,128)S(1)} fusion(f32[1024,256]{0,1:T(8,128)S(1)} %fusion.120, f32[5,1024]{1,0:T(8,128)S(1)} %dynamic-slice_bitcast_fusion.5, f32[5,256,128]{2,1,0:T(8,128)S(1)} %get-tuple-element.458, pred[]{:T(512)S(6)} %compare.32, s32[1024]{0:T(1024)S(1)} %bitcast.198), kind=kOutput, calls=%fused_computation.35.clone.1 | convolution fusion | flops 2015035392 | bytes 2383873 | tf_op jit(solution)/shard_map/while/body/eval_jaxpr/kph,pl->khl/dot_general | solution.py:215
  213.5 3.1 %fusion.121 = f32[5,256,128]{2,1,0:T(8,128)S(1)} fusion(f32[1024,256]{0,1:T(8,128)S(1)} %fusion.120, f32[5,1024]{1,0:T(8,128)S(1)} %dynamic-slice_bitcast_fusion.5, f32[5,256,128]{2,1,0:T(8,128)S(1)} %get-tuple-element.458, pred[]{:T(512)S(6)} %compare.32, s32[1024]{0:T(1024)S(1)} %bitcast.198), kind=kOutput, calls=%fused_computation.35.clone.1 | convolution fusion | flops 2015035392 | bytes 2383873 | tf_op jit(solution)/shard_map/while/body/eval_jaxpr/kph,pl->khl/dot_general | solution.py:215
  216.7 3.1 %fusion.121 = f32[5,256,128]{2,1,0:T(8,128)S(1)} fusion(f32[1024,256]{0,1:T(8,128)S(1)} %fusion.120, f32[5,1024]{1,0:T(8,128)S(1)} %dynamic-slice_bitcast_fusion.5, f32[5,256,128]{2,1,0:T(8,128)S(1)} %get-tuple-element.458, pred[]{:T(512)S(6)} %compare.32, s32[1024]{0:T(1024)S(1)} %bitcast.198), kind=kOutput, calls=%fused_computation.35.clone.1 | convolution fusion | flops 2015035392 | bytes 2383873 | tf_op jit(solution)/shard_map/while/body/eval_jaxpr/kph,pl->khl/dot_general | solution.py:215
  222.7 3.9 %collective-permute-start.5 = (f32[5,32,8,1]{1,2,3,0:T(8,128)S(1)}, f32[5,32,8,1]{1,2,3,0:T(8,128)S(1)}, u32[]{:S(2)}, u32[]{:S(2)}) collective-permute-start(f32[5,32,8,1]{1,2,3,0:T(8,128)S(1)} %copy.91), channel_id=1, source_target_pairs={{32,0},{64,32},{96,64},{33,1},{65,33},{97,65},{34,2},{66,34},{98,6... | collective-permute-start | bytes 15368 | tf_op jit(solution)/shard_map/ppermute | solution.py:33
  228.6 2.4 %collective-permute-start.7 = (f32[5,32,1,128]{3,2,1,0:T(1,128)S(1)}, f32[5,32,1,128]{3,2,1,0:T(1,128)S(1)}, u32[]{:S(2)}, u32[]{:S(2)}) collective-permute-start(f32[5,32,1,128]{3,2,1,0:T(1,128)S(1)} %get-tuple-element.239), channel_id=1, source_target_pairs={{0,1},{1,2},{2,3},{3,4},{4,5},{5,6},{6,7},{7,8},{8,9},{9,10},{10,1... | collective-permute-start | bytes 245768 | tf_op jit(solution)/shard_map/ppermute | solution.py:32
  232.4 4.0 %collective-permute-done.7 = f32[5,32,1,128]{3,2,1,0:T(1,128)S(1)} collective-permute-done((f32[5,32,1,128]{3,2,1,0:T(1,128)S(1)}, f32[5,32,1,128]{3,2,1,0:T(1,128)S(1)}, u32[]{:S(2)}, u32[]{:S(2)}) %collective-permute-start.7) | collective-permute-done | bytes 81952 | tf_op jit(solution)/shard_map/ppermute | solution.py:32
  (174 shorter events, 30.0 us)
Async XLA Ops:
  2.8 21.9 %copy-start.6 = (s32[8192]{0:T(1024)S(1)}, s32[8192]{0:T(1024)}, u32[]{:S(2)}) copy-start(s32[8192]{0:T(1024)} %param.23) | copy-start | bytes 98308
  2.8 22.7 %copy-start = (f32[4,32,8,128]{3,2,1,0:T(8,128)S(1)}, f32[4,32,8,128]{3,2,1,0:T(8,128)}, u32[]{:S(2)}) copy-start(f32[4,32,8,128]{3,2,1,0:T(8,128)} %param.18) | copy-start | bytes 1572868
  2.8 22.7 %collective-permute-start = (f32[4,32,8,1]{3,2,1,0:T(8,128)}, f32[4,32,8,1]{3,2,1,0:T(8,128)S(1)}, u32[]{:S(2)}, u32[]{:S(2)}) collective-permute-start(f32[4,32,8,1]{3,2,1,0:T(8,128)} %get-tuple-element.247), channel_id=1, source_target_pairs={{0,32},{32,64},{64,96},{1,33},{33,65},{65,97},{2,34},{34,66},{66,9... | collective-permute-start | bytes 12296 | tf_op jit(solution)/shard_map/ppermute | solution.py:32
  6.5 19.1 %collective-permute-start.1 = (f32[4,32,8,1]{3,2,1,0:T(8,128)S(1)}, f32[4,32,8,1]{3,2,1,0:T(8,128)S(1)}, u32[]{:S(2)}, u32[]{:S(2)}) collective-permute-start(f32[4,32,8,1]{3,2,1,0:T(8,128)S(1)} %get-tuple-element.246), channel_id=1, source_target_pairs={{32,0},{64,32},{96,64},{33,1},{65,33},{97,65},{34,2},{66,34},{98,6... | collective-permute-start | bytes 12296 | tf_op jit(solution)/shard_map/ppermute | solution.py:33
  10.8 14.8 %collective-permute-start.2 = (f32[4,32,1,128]{3,2,1,0:T(1,128)}, f32[4,32,1,128]{3,2,1,0:T(1,128)S(1)}, u32[]{:S(2)}, u32[]{:S(2)}) collective-permute-start(f32[4,32,1,128]{3,2,1,0:T(1,128)} %get-tuple-element.244), channel_id=1, source_target_pairs={{1,0},{2,1},{3,2},{4,3},{5,4},{6,5},{7,6},{8,7},{9,8},{10,9},{11,1... | collective-permute-start | bytes 196616 | tf_op jit(solution)/shard_map/ppermute | solution.py:33
  15.6 10.0 %collective-permute-start.3 = (f32[4,32,1,128]{3,2,1,0:T(1,128)}, f32[4,32,1,128]{3,2,1,0:T(1,128)S(1)}, u32[]{:S(2)}, u32[]{:S(2)}) collective-permute-start(f32[4,32,1,128]{3,2,1,0:T(1,128)} %get-tuple-element.245), channel_id=1, source_target_pairs={{0,1},{1,2},{2,3},{3,4},{4,5},{5,6},{6,7},{7,8},{8,9},{9,10},{10,1... | collective-permute-start | bytes 196616 | tf_op jit(solution)/shard_map/ppermute | solution.py:32
  26.3 19.0 %copy-start.2 = (f32[6,8192]{1,0:T(8,128)S(1)}, f32[6,8192]{1,0:T(8,128)}, u32[]{:S(2)}) copy-start(f32[6,8192]{1,0:T(8,128)} %param.20) | copy-start | bytes 589828
  26.4 19.0 %copy-start.3 = (f32[3,8192]{1,0:T(4,128)S(1)}, f32[3,8192]{1,0:T(4,128)}, u32[]{:S(2)}) copy-start(f32[3,8192]{1,0:T(4,128)} %param.19) | copy-start | bytes 294916
  26.4 19.0 %copy-start.4 = (f32[8192]{0:T(1024)S(1)}, f32[8192]{0:T(1024)}, u32[]{:S(2)}) copy-start(f32[8192]{0:T(1024)} %param.21) | copy-start | bytes 98308
  26.4 19.0 %copy-start.7 = (f32[8192]{0:T(1024)S(1)}, f32[8192]{0:T(1024)}, u32[]{:S(2)}) copy-start(f32[8192]{0:T(1024)} %param.22) | copy-start | bytes 98308
  45.3 0.8 copy-start.1
  129.8 13.6 %copy-start.8 = (f32[3]{0:T(128)S(1)}, f32[3]{0:T(128)}, u32[]{:S(2)}) copy-start(f32[3]{0:T(128)} %constant.127) | copy-start | bytes 40
  145.0 25.7 %all-to-all-start.2 = ((f32[10,128,128]{2,0,1:T(8,128)}), f32[10,128,128]{2,0,1:T(8,128)S(1)}, u32[]{:S(2)}, u32[]{:S(2)}) async-start(f32[10,128,128]{2,0,1:T(8,128)} %copy.88), calls=%async_computation.2 | async-start | bytes 2097152 | tf_op jit(solution)/shard_map/all_to_all | solution.py:194
  170.9 22.6 %copy-start.5 = (f32[8192]{0:T(1024)S(1)}, f32[8192]{0:T(1024)}, u32[]{:S(2)}) copy-start(f32[8192]{0:T(1024)} %param.21) | copy-start | bytes 98308
  220.5 11.3 %collective-permute-start.4 = (f32[5,32,8,1]{1,2,3,0:T(8,128)S(1)}, f32[5,32,8,1]{1,2,3,0:T(8,128)S(1)}, u32[]{:S(2)}, u32[]{:S(2)}) collective-permute-start(f32[5,32,8,1]{1,2,3,0:T(8,128)S(1)} %copy.90), channel_id=1, source_target_pairs={{0,32},{32,64},{64,96},{1,33},{33,65},{65,97},{2,34},{34,66},{66,9... | collective-permute-start | bytes 15368 | tf_op jit(solution)/shard_map/ppermute | solution.py:32
  222.7 9.4 %collective-permute-start.5 = (f32[5,32,8,1]{1,2,3,0:T(8,128)S(1)}, f32[5,32,8,1]{1,2,3,0:T(8,128)S(1)}, u32[]{:S(2)}, u32[]{:S(2)}) collective-permute-start(f32[5,32,8,1]{1,2,3,0:T(8,128)S(1)} %copy.91), channel_id=1, source_target_pairs={{32,0},{64,32},{96,64},{33,1},{65,33},{97,65},{34,2},{66,34},{98,6... | collective-permute-start | bytes 15368 | tf_op jit(solution)/shard_map/ppermute | solution.py:33
  226.6 5.8 %collective-permute-start.6 = (f32[5,32,1,128]{3,2,1,0:T(1,128)S(1)}, f32[5,32,1,128]{3,2,1,0:T(1,128)S(1)}, u32[]{:S(2)}, u32[]{:S(2)}) collective-permute-start(f32[5,32,1,128]{3,2,1,0:T(1,128)S(1)} %get-tuple-element.238), channel_id=1, source_target_pairs={{1,0},{2,1},{3,2},{4,3},{5,4},{6,5},{7,6},{8,7},{9,8},{10,9},{11,1... | collective-permute-start | bytes 245768 | tf_op jit(solution)/shard_map/ppermute | solution.py:33
  228.6 7.9 %collective-permute-start.7 = (f32[5,32,1,128]{3,2,1,0:T(1,128)S(1)}, f32[5,32,1,128]{3,2,1,0:T(1,128)S(1)}, u32[]{:S(2)}, u32[]{:S(2)}) collective-permute-start(f32[5,32,1,128]{3,2,1,0:T(1,128)S(1)} %get-tuple-element.239), channel_id=1, source_target_pairs={{0,1},{1,2},{2,3},{3,4},{4,5},{5,6},{6,7},{7,8},{8,9},{9,10},{10,1... | collective-permute-start | bytes 245768 | tf_op jit(solution)/shard_map/ppermute | solution.py:32
where the time goes:
time: 240 us; the launch traced here: 239 us
  matrix products  116 us (48%)
  starting transfers between devices  30.3 us (13%)
  other arithmetic  28.8 us (12%)
  blocking collectives  28.8 us (12%)
  waiting for transfers between devices  22.2 us (9%)
  local copies, waits for them, and re-layouts  10.5 us (4%)
    dot_general x8, matrix products, place(): jnp.einsum('cpo,pr->cor', weighted, one_hot(ranks, peer_slots, jnp.float3...  36.3 us
    all_to_all x2, blocking collectives, turned_blocks(): lax.all_to_all(pieces, axes[k], split_axis=k, concat_axis=k, tiled=True)  28.8 us
    dot_general x8, matrix products, deposit(): jnp.einsum('kph,pl->khl', weighted, one_hot(low_ids, grid_cols, jnp.float...  24.6 us
    dot_general x8, matrix products, fetch(): jnp.einsum('cor,pr->cpo', returned, one_hot(ranks, peer_slots, jnp.float3...  20.6 us
    all_to_all x1, waiting for transfers between devices, shards(): lax.all_to_all(result, GX_GY, split_axis=1, concat_axis=1, tiled=True)  18.2 us
    dot_general x8, matrix products, look_up(): jnp.einsum('khl,pl->kph', filtered, one_hot(low_ids, grid_cols, jnp.float...  17.4 us
    reduce_sum x1, other arithmetic, contact(): weight_sum = jnp.sum(weight, axis=2)  16.1 us
    dot_general x1, matrix products, contact(): jnp.einsum('bij,cbj->cbi', weight, stacked, precision=lax.Precision.HIGHEST)  13.3 us
  transfers between devices with their start and end apart: 9, of which 2 were waited for; matrix products, arithmetic and copies ran while one was open for 5% of the time, Pallas kernels for 0%

commit v1 on v0

v1 whole, which is shorter than its diff:
```python
import functools

import jax
import jax.numpy as jnp
from jax import lax
from jax.experimental import pallas as pl
from jax.experimental.pallas import tpu as pltpu
from jax.sharding import PartitionSpec as P

GX_GY = ("gx", "gy")
LOGICAL = pl.DeviceIdType.LOGICAL
F32, BF16, I32 = jnp.float32, jnp.bfloat16, jnp.int32
DEV = 128
PARTS = 8192
PB = 256
NBLK = PARTS // PB
LOG2E = 1.4426950408889634
VMEM = pltpu.VMEM


def iota(shape, dim):
    return lax.broadcasted_iota(I32, shape, dim)


def hot(mask):
    return jnp.where(mask, 1.0, 0.0).astype(BF16)


def split2(x):
    hi = x.astype(BF16)
    lo = (x - hi.astype(F32)).astype(BF16)
    return hi, lo


def dot_nt(a, b):
    return lax.dot_general(a, b, (((1,), (1,)), ((), ())), preferred_element_type=F32)


def dot_nn(a, b):
    return lax.dot_general(a, b, (((1,), (0,)), ((), ())), preferred_element_type=F32)


def dot_tn(a, b):
    return lax.dot_general(a, b, (((0,), (0,)), ((), ())), preferred_element_type=F32)


def row2(ref, k):
    return jnp.concatenate([ref[pl.ds(2 * k, 1), :], ref[pl.ds(2 * k + 1, 1), :]], axis=1)


def add2(ref, x):
    ref[0] += x[:, :128]
    ref[1] += x[:, 128:]


def place_kernel(
    owner_ref, box_ref, pos_ref, mot_ref, rad_ref, tmp_ref,
    out_ref, q_ref, sc_ref,
    rank_ref, acc_ref, sorted_ref, cnt_ref, smem_ref, sem,
):
    tri = hot(iota((PB, PB), 0) < iota((PB, PB), 1))

    def rank_step(k, before):
        box = row2(box_ref, k)
        match = iota((DEV, PB), 0) == box
        h = hot(match)
        within = dot_nn(h, tri)
        rank = jnp.sum(jnp.where(match, within + before, 0.0), axis=0, keepdims=True)
        rank_ref[pl.ds(2 * k, 1), :] = rank[:, :128]
        rank_ref[pl.ds(2 * k + 1, 1), :] = rank[:, 128:]
        return before + jnp.sum(jnp.where(match, 1.0, 0.0), axis=1, keepdims=True)

    counts = lax.fori_loop(0, NBLK, rank_step, jnp.zeros((DEV, 1), F32))
    wide = jnp.broadcast_to(counts, (DEV, DEV))
    lower = iota((DEV, DEV), 0) < iota((DEV, DEV), 1)
    start_row = jnp.sum(jnp.where(lower, wide, 0.0), axis=0, keepdims=True)
    diag = iota((DEV, DEV), 0) == iota((DEV, DEV), 1)
    count_row = jnp.sum(jnp.where(diag, wide, 0.0), axis=0, keepdims=True)
    sc = jnp.where(iota((8, DEV), 0) == 0, start_row, count_row).astype(I32)
    cnt_ref[...] = sc
    copy = pltpu.make_async_copy(cnt_ref, smem_ref, sem)
    copy.start()
    sc_ref[...] = sc
    table = jnp.broadcast_to(start_row, (64, DEV))
    q = rank_ref[...] + jnp.take_along_axis(table, box_ref[...], axis=1)
    q_ref[...] = q.astype(I32)

    acc_ref[...] = jnp.zeros_like(acc_ref)

    def sort_step(k, carry):
        q = row2(q_ref, k)
        lo_hot = hot(iota((PB, PB), 0) == (q & 255))
        hi_hot = hot(iota((32, PB), 0) == (q >> 8))
        lanes = pl.ds(pl.multiple_of(k * PB, PB), PB)
        rows = [pos_ref[c : c + 1, lanes] for c in range(3)]
        rows += [row2(tmp_ref, k)]
        rows += [mot_ref[c : c + 1, lanes] for c in range(3)]
        rows += [row2(rad_ref, k)]
        rows += [mot_ref[c : c + 1, lanes] for c in range(3, 6)]
        his, los = [], []
        for x in rows:
            hi, lo = split2(jnp.broadcast_to(x, (32, PB)))
            his.append(hi * hi_hot)
            los.append(lo * hi_hot)
        left = jnp.concatenate(
            [jnp.concatenate(his, axis=0), jnp.concatenate(los, axis=0)], axis=1
        )
        right = jnp.concatenate([lo_hot, lo_hot], axis=1)
        add2(acc_ref, dot_nt(left, right))
        return carry

    lax.fori_loop(0, NBLK, sort_step, 0)
    for t in range(64):
        sorted_ref[t, 0:11, :] = acc_ref[t % 2, pl.ds(t // 2, 11, stride=32), :]
    copy.wait()
    lane = iota((16, 128), 1)

    def window(b, carry):
        start = smem_ref[0, b]
        count = smem_ref[1, b]
        tile, off = start >> 7, start & 127
        shift = (128 - off) & 127
        low = pltpu.roll(sorted_ref[tile], shift, 1)
        high = pltpu.roll(sorted_ref[tile + 1], shift, 1)
        both = jnp.where(lane < 128 - off, low, high)
        out_ref[owner_ref[b]] = jnp.where(lane < count, both, 0.0)
        return carry

    lax.fori_loop(0, DEV, window, 0, unroll=4)


def place(box_owner, box, pos, mot, rad, tmp):
    return pl.pallas_call(
        place_kernel,
        out_shape=(
            jax.ShapeDtypeStruct((DEV, 16, 128), F32),
            jax.ShapeDtypeStruct((64, 128), I32),
            jax.ShapeDtypeStruct((8, 128), I32),
        ),
        in_specs=[pl.BlockSpec(memory_space=pltpu.SMEM)] + [pl.BlockSpec(memory_space=VMEM)] * 5,
        out_specs=(pl.BlockSpec(memory_space=VMEM),) * 3,
        scratch_shapes=[
            VMEM((64, 128), F32),
            VMEM((2, 352, 128), F32),
            VMEM((66, 16, 128), F32),
            VMEM((8, 128), I32),
            pltpu.SMEM((8, 128), I32),
            pltpu.SemaphoreType.DMA,
        ],
        name="place",
    )(box_owner, box, pos, mot, rad, tmp)


def contact_block(s, mask):
    sub = iota((8, 128), 0)
    top = s[0:8]
    r = s[7:8]
    occupied = jnp.where(r > 0.0, 1.0, 0.0)
    scale = jnp.where((sub & 3) == 3, 1.4142135623730951, (2.0 * LOG2E) ** 0.5)
    pos4 = jnp.concatenate([s[0:3], r, s[0:3], r], axis=0)
    y = pos4 * scale
    a = y.astype(BF16).astype(F32)
    b = (y - a).astype(BF16).astype(F32)
    c = y - a - b
    first = sub < 4
    is_r = (sub & 3) == 3
    sq = y * y * 0.5
    m = jnp.sum(jnp.where(first & ~is_r, sq, 0.0), axis=0, keepdims=True)
    g = sq[3:4] + 0.5

    def three(v):
        v1 = v.astype(BF16).astype(F32)
        v2 = (v - v1).astype(BF16).astype(F32)
        return v1, v2, v - v1 - v2

    m1, m2, m3 = three(m)
    g1, g2, g3 = three(g)

    def pick(rows):
        out = jnp.zeros((8, 128), F32)
        for i, v in enumerate(rows):
            out = jnp.where(sub == i, v, out)
        return out

    zero = jnp.zeros((8, 128), F32)
    left = jnp.concatenate(
        [a, b, jnp.where(first, a, c), pick([m1, m2, m3, 1.0, 1.0, 1.0]), pick([g1, g2, g3, 1.0, 1.0, 1.0]), zero], axis=0
    ).astype(BF16)
    h1 = jnp.where(first, a, b)
    h3 = jnp.where(first, c, a)
    h4 = pick([-1.0, -1.0, -1.0, -m1, -m2, -m3])
    h5 = pick([1.0, 1.0, 1.0, g1, g2, g3])
    e_cols = jnp.concatenate(
        [jnp.where(is_r, 0.0, h1), jnp.where(is_r, 0.0, h1), jnp.where(is_r, 0.0, h3), h4, zero, zero], axis=0
    )
    r_cols = jnp.concatenate(
        [jnp.where(is_r, h1, 0.0), jnp.where(is_r, h1, 0.0), jnp.where(is_r, h3, 0.0), zero, h5, zero], axis=0
    )
    right = jnp.concatenate([e_cols, r_cols], axis=1).astype(BF16)
    pair = dot_tn(left, right)
    weight = jnp.where(mask != 0, jnp.exp2(pair[:, :128] / pair[:, 128:]), 0.0)
    wh, wl = split2(weight)
    top_o = jnp.where(sub == 7, occupied, top)
    stacked = jnp.concatenate([top_o, s[8:16]], axis=0)
    sh, sl = split2(stacked)
    lhs = jnp.concatenate(
        [jnp.concatenate([sh, sh], axis=1), jnp.concatenate([sl, jnp.zeros_like(sl)], axis=1)], axis=0
    )
    mixed = dot_nt(lhs, jnp.concatenate([wh, wl], axis=1))
    mixed = mixed[0:16] + mixed[16:32]
    ws = mixed[7:8]
    diff = top * ws - mixed[0:8]
    c1 = jnp.where(sub == 3, -0.03, 0.05)
    c2 = jnp.where(sub == 3, 0.0, 0.02)
    spin = s[8:16] - 0.01 * (s[8:16] * ws + mixed[8:16])
    return jnp.where(first, c1 * diff - c2 * pltpu.roll(diff, 4, 0), pltpu.roll(spin, 4, 0))


def contact_kernel(
    out_ref, mask_hbm, ret_ref,
    got_ref, res_ref, mask_ref, send_sem, got_sem, back_sem, ret_sem, mask_sem,
):
    me = lax.axis_index("gx") * 32 + lax.axis_index("gy")

    def mask_copy(i):
        part = pl.ds(16 * i, 16)
        return pltpu.make_async_copy(mask_hbm.at[part], mask_ref.at[part], mask_sem.at[i])

    for i in range(8):
        mask_copy(i).start()
    barrier = pltpu.get_barrier_semaphore()

    def signal(d, carry):
        pl.semaphore_signal(barrier, inc=1, device_id=lax.rem(me + d, DEV), device_id_type=LOGICAL)
        return carry

    lax.fori_loop(1, DEV, signal, 0)
    pl.semaphore_wait(barrier, DEV - 1)

    def send(d):
        peer = lax.rem(me + d, DEV)
        return pltpu.make_async_remote_copy(
            out_ref.at[peer, pl.ds(0, 11)], got_ref.at[me, pl.ds(0, 11)],
            send_sem.at[d], got_sem.at[me], device_id=peer, device_id_type=LOGICAL,
        )

    def got(d):
        peer = lax.rem(me + DEV - d, DEV)
        return pltpu.make_async_remote_copy(
            out_ref.at[peer, pl.ds(0, 11)], got_ref.at[peer, pl.ds(0, 11)],
            send_sem.at[d], got_sem.at[peer], device_id=peer, device_id_type=LOGICAL,
        )

    def back(d):
        peer = lax.rem(me + DEV - d, DEV)
        return pltpu.make_async_remote_copy(
            res_ref.at[peer, pl.ds(0, 7)], ret_ref.at[me, pl.ds(0, 7)],
            back_sem.at[d], ret_sem.at[me], device_id=peer, device_id_type=LOGICAL,
        )

    def returned(d):
        peer = lax.rem(me + d, DEV)
        return pltpu.make_async_remote_copy(
            res_ref.at[peer, pl.ds(0, 7)], ret_ref.at[peer, pl.ds(0, 7)],
            back_sem.at[d], ret_sem.at[peer], device_id=peer, device_id_type=LOGICAL,
        )

    def start_send(d, carry):
        send(d).start()
        return carry

    lax.fori_loop(1, DEV, start_send, 0)
    for i in range(8):
        mask_copy(i).wait()
    tail = jnp.zeros((5, 128), F32)
    ret_ref[me] = contact_block(out_ref[me], mask_ref[me])

    def step(d, carry):
        peer = lax.rem(me + DEV - d, DEV)
        got(d).wait_recv()
        s = jnp.concatenate([got_ref[peer, 0:11, :], tail], axis=0)
        res_ref[peer] = contact_block(s, mask_ref[peer])

        @pl.when(d > 1)
        def _():
            back(d - 1).start()

        return carry

    lax.fori_loop(1, DEV, step, 0)
    back(DEV - 1).start()

    def finish(d, carry):
        send(d).wait_send()
        back(d).wait_send()
        returned(d).wait_recv()
        return carry

    lax.fori_loop(1, DEV, finish, 0)


def exchange(outgoing, mask):
    return pl.pallas_call(
        contact_kernel,
        out_shape=jax.ShapeDtypeStruct((DEV, 8, 128), F32),
        in_specs=[pl.BlockSpec(memory_space=VMEM), pl.BlockSpec(memory_space=pl.ANY)],
        out_specs=pl.BlockSpec(memory_space=VMEM),
        scratch_shapes=[
            VMEM((DEV, 16, 128), F32),
            VMEM((DEV, 8, 128), F32),
            VMEM((DEV, 128, 128), I32),
            pltpu.SemaphoreType.DMA((DEV,)),
            pltpu.SemaphoreType.DMA((DEV,)),
            pltpu.SemaphoreType.DMA((DEV,)),
            pltpu.SemaphoreType.DMA((DEV,)),
            pltpu.SemaphoreType.DMA((8,)),
        ],
        compiler_params=pltpu.CompilerParams(collective_id=0, has_side_effects=True),
        name="exchange",
    )(outgoing, mask)


def gather_kernel(field_ref, cell_ref, seen_ref, f_ref):
    for c in range(4):
        ft = jnp.transpose(field_ref[c])
        hi, lo = split2(ft)
        f_ref[pl.ds(128 * c, 128), 0:256] = hi
        f_ref[pl.ds(128 * c, 128), 256:512] = lo

    def step(k, carry):
        cell = row2(cell_ref, k)
        high = hot(iota((256, PB), 0) == (cell >> 7))
        part = dot_nn(f_ref[...], jnp.concatenate([high, high], axis=0))
        low = iota((128, PB), 0) == (cell & 127)
        rows = [
            jnp.sum(jnp.where(low, part[128 * c : 128 * c + 128], 0.0), axis=0, keepdims=True)
            for c in range(4)
        ]
        seen_ref[:, pl.ds(pl.multiple_of(k * PB, PB), PB)] = jnp.concatenate(rows, axis=0)
        return carry

    lax.fori_loop(0, NBLK, step, 0)


def gather(field, cell):
    return pl.pallas_call(
        gather_kernel,
        out_shape=jax.ShapeDtypeStruct((4, PARTS), F32),
        in_specs=[pl.BlockSpec(memory_space=VMEM)] * 2,
        out_specs=pl.BlockSpec(memory_space=VMEM),
        scratch_shapes=[VMEM((512, 512), BF16)],
        name="gather",
    )(field, cell)


def finish_kernel(
    owner_ref, sc_ref, q_ref, cell_ref, ret_ref, seen_ref, mot_ref, rad_ref, tmp_ref,
    next_ref, dep_ref,
    dense_ref, left_ref, acc_ref,
):
    lane = iota((8, 128), 1)

    def pack(b, carry):
        start = sc_ref[0, b]
        tile, off = start >> 7, start & 127
        mine = pltpu.roll(ret_ref[owner_ref[b]], off, 1)
        dense_ref[tile] = jnp.where(lane < off, dense_ref[tile], mine)
        dense_ref[tile + 1] = mine
        return carry

    lax.fori_loop(0, DEV, pack, 0, unroll=2)
    hi, lo = split2(dense_ref[0:64].reshape(512, 128))
    left_ref[:, 0:128] = hi
    left_ref[:, 128:256] = lo
    acc_ref[...] = jnp.zeros_like(acc_ref)

    def step(k, carry):
        lanes = pl.ds(pl.multiple_of(k * PB, PB), PB)
        q = row2(q_ref, k)
        low = hot(iota((128, PB), 0) == (q & 127))
        part = dot_nn(left_ref[...], jnp.concatenate([low, low], axis=0))
        high = jnp.broadcast_to(q >> 7, (8, PB))
        res = part[0:8]
        for t in range(1, 64):
            res = jnp.where(high == t, part[8 * t : 8 * t + 8], res)
        r = row2(rad_ref, k)
        temp = row2(tmp_ref, k)
        u = seen_ref[0:3, lanes]
        gas = seen_ref[3:4, lanes]
        v = mot_ref[0:3, lanes]
        drag = 4.0 / (r * r + 0.25) * (u - v)
        vn = v + (res[0:3] + 0.1 * drag) - jnp.where(iota((3, PB), 0) == 2, 0.03, 0.0)
        tn = temp + (res[3:4] + 0.4 * (gas - temp))
        next_ref[0:3, lanes] = vn
        next_ref[3:6, lanes] = res[4:7]
        next_ref[6:7, lanes] = tn
        volume = r * r * r
        push = -volume * drag
        rows = [volume, push[0:1], push[1:2], push[2:3], volume * (tn - gas)]
        cell = row2(cell_ref, k)
        lo_hot = hot(iota((256, PB), 0) == (cell & 255))
        hi_hot = hot(iota((128, PB), 0) == (cell >> 8))
        his, los = [], []
        for x in rows:
            hi, lo = split2(jnp.broadcast_to(x, (128, PB)))
            his.append(hi * hi_hot)
            los.append(lo * hi_hot)
        left = jnp.concatenate(
            [jnp.concatenate(his, axis=0), jnp.concatenate(los, axis=0)], axis=1
        )
        add2(acc_ref, dot_nt(left, jnp.concatenate([lo_hot, lo_hot], axis=1)))
        return carry

    lax.fori_loop(0, NBLK, step, 0)
    for f in range(5):
        for j in range(2):
            dep_ref[f, pl.ds(j, 128, stride=2), :] = acc_ref[j, pl.ds(128 * f, 128), :]


def finish(owner, sc, q, cell, ret, seen, mot, rad, tmp):
    return pl.pallas_call(
        finish_kernel,
        out_shape=(
            jax.ShapeDtypeStruct((7, PARTS), F32),
            jax.ShapeDtypeStruct((5, 256, 128), F32),
        ),
        in_specs=[pl.BlockSpec(memory_space=pltpu.SMEM)] * 2 + [pl.BlockSpec(memory_space=VMEM)] * 7,
        out_specs=(pl.BlockSpec(memory_space=VMEM),) * 2,
        scratch_shapes=[
            VMEM((66, 8, 128), F32),
            VMEM((512, 256), BF16),
            VMEM((2, 640, 128), F32),
        ],
        name="finish",
    )(owner, sc, q, cell, ret, seen, mot, rad, tmp)


def with_halo(value, sides):
    edges = {}
    for axis, dim in sides:
        size, length = (lax.axis_size(axis), value.shape[dim])
        up = [(i, i + 1) for i in range(size - 1)]
        last = lax.slice_in_dim(value, length - 1, length, axis=dim)
        first = lax.slice_in_dim(value, 0, 1, axis=dim)
        edges[dim] = (
            lax.ppermute(last, axis, up),
            lax.ppermute(first, axis, [(b, a) for a, b in up]),
        )
    done = []
    for _, dim in sides:
        low, high = edges[dim]
        around = [(1, 1) if d in done else (0, 0) for d in range(value.ndim)]
        value = jnp.concatenate([jnp.pad(low, around), value, jnp.pad(high, around)], axis=dim)
        done.append(dim)
    return value


def stencil(padded):
    interior = padded[:, :, 1:-1, 1:-1]
    z_padded = jnp.pad(interior, ((0, 0), (1, 1), (0, 0), (0, 0)))
    beside_all = z_padded[:, 2:] + z_padded[:, :-2]
    beside_all = beside_all + padded[:, :, 2:, 1:-1] + padded[:, :, :-2, 1:-1]
    beside_all = beside_all + padded[:, :, 1:-1, 2:] + padded[:, :, 1:-1, :-2]
    return 0.25 * interior + 0.125 * beside_all


def shards(fluid, pos, mot, rad, tmp, cell, box, box_owner, mask):
    rad2, tmp2 = rad.reshape(64, 128), tmp.reshape(64, 128)
    cell2, box2 = cell.reshape(64, 128), box.reshape(64, 128)
    filtered = stencil(with_halo(fluid, (("gx", 3), ("gy", 2))))
    seen = gather(filtered.reshape(4, 256, 128), cell2)
    outgoing, q, sc = place(box_owner, box2, pos, mot, rad2, tmp2)
    ret = exchange(outgoing, mask)
    nxt, dep = finish(box_owner, sc, q, cell2, ret, seen, mot, rad2, tmp2)
    spread = stencil(with_halo(dep.reshape(5, 32, 8, 128), (("gx", 3), ("gy", 2))))
    crowding = 1.0 + 4.0 * spread[0]
    fluid_next = fluid + 0.4 * spread[1:5] * crowding
    return fluid_next, 1.0 / crowding, nxt


def solution(mesh):
    return jax.shard_map(
        shards,
        mesh=mesh,
        in_specs=(
            P(None, None, "gy", "gx"),
            P(None, GX_GY),
            P(None, GX_GY),
            P(GX_GY),
            P(GX_GY),
            P(GX_GY),
            P(GX_GY, None),
            P(),
            P(GX_GY, None, None),
        ),
        out_specs=(P(None, None, "gy", "gx"), P(None, "gy", "gx"), P(None, GX_GY)),
        check_vma=False,
    )
```

time: 240 us -> 168 us (0.70)
  the two profiles are of different devices: /device:TPU:10 before, /device:TPU:0 now
where the time goes in v1:
time: 168 us; the launch traced here: 166 us
  Pallas kernels  129 us (77%)
  starting transfers between devices  21 us (12%)
  local copies, waits for them, and re-layouts  7.01 us (4%)
  other arithmetic  6.96 us (4%)
    pallas_call x1, Pallas kernels, exchange(): pl.pallas_call(contact_kernel, out_shape=jax.ShapeDtypeStruct((DEV, 8, 12...  73.7 us
    pallas_call x1, Pallas kernels, finish(): pl.pallas_call(finish_kernel, out_shape=(jax.ShapeDtypeStruct((7, PARTS),...  23.2 us
    pallas_call x1, Pallas kernels, place(): pl.pallas_call(place_kernel, out_shape=(jax.ShapeDtypeStruct((DEV, 16, 12...  20.5 us
    ppermute x4, starting transfers between devices, with_halo(): lax.ppermute(last, axis, up)  15.9 us
    pallas_call x1, Pallas kernels, gather(): pl.pallas_call(gather_kernel, out_shape=jax.ShapeDtypeStruct((4, PARTS),...  11.7 us
    slice x4, local copies, waits for them, and re-layouts, with_halo(): first = lax.slice_in_dim(value, 0, 1, axis=dim)  5.69 us
    ppermute x4, starting transfers between devices, with_halo(): lax.ppermute(first, axis, [(b, a) for a, b in up])  5.16 us
    add x1, other arithmetic, stencil(): return 0.25 * interior + 0.125 * beside_all  3.88 us
  transfers between devices with their start and end apart: 8, of which 1 were waited for; matrix products, arithmetic and copies ran while one was open for 3% of the time, Pallas kernels for 57%

profile of v1, /device:TPU:0, one launch (start us, length us, event | category | flops | bytes accessed | tf_op | source)
XLA Modules:
  0.0 166.1 jit_solution(11078375380286854787)
XLA Ops:
  0.6 0.0 copy-start
  0.6 1.4 fusion.23
  2.0 1.3 collective-permute-start.2
  3.3 3.0 %collective-permute-start.3 = (f32[4,32,1,128]{3,2,1,0:T(1,128)S(1)}, f32[4,32,1,128]{3,2,1,0:T(1,128)S(1)}, u32[]{:S(2)}, u32[]{:S(2)}) collective-permute-start(f32[4,32,1,128]{3,2,1,0:T(1,128)S(1)} %get-tuple-element.20), channel_id=1, source_target_pairs={{0,1},{1,2},{2,3},{3,4},{4,5},{5,6},{6,7},{7,8},{8,9},{9,10},{10,1... | collective-permute-start | bytes 196616 | tf_op jit(solution)/shard_map/ppermute | solution.py:446
  6.3 1.4 fusion.24
  7.7 1.3 collective-permute-start.1
  9.0 4.6 %collective-permute-start = (f32[4,32,8,1]{3,2,1,0:T(8,128)S(1)}, f32[4,32,8,1]{3,2,1,0:T(8,128)S(1)}, u32[]{:S(2)}, u32[]{:S(2)}) collective-permute-start(f32[4,32,8,1]{3,2,1,0:T(8,128)S(1)} %get-tuple-element.22), channel_id=1, source_target_pairs={{0,32},{32,64},{64,96},{1,33},{33,65},{65,97},{2,34},{34,66},{66,9... | collective-permute-start | bytes 12296 | tf_op jit(solution)/shard_map/ppermute | solution.py:446
  13.6 20.5 %place.1 = (f32[128,16,128]{2,1,0:T(8,128)}, s32[64,128]{1,0:T(8,128)}, s32[8,128]{1,0:T(8,128)}) custom-call(s32[128]{0:T(128)} %owner_ref.3, s32[64,128]{1,0:T(8,128)} %bitcast.20, f32[3,8192]{1,0:T(4,128)} %pos_ref.1, f32[6,8192]{1,0:T(8,128)} %mot_ref.3, f32[64,128]{1,0:T(8,128)} %bitcast.14, f32[64,128]{1,0:T(8,128)} %bitcast.16), custom_call_target="tpu_custom_call" | custom-call | tf_op jit(solution)/shard_map/place/pallas_call | solution.py:133
  34.1 73.7 %exchange.1.ret_ref = f32[128,8,128]{2,1,0:T(8,128)} custom-call(f32[128,16,128]{2,1,0:T(8,128)} %get-tuple-element.10.out_ref, s32[128,128,128]{2,1,0:T(8,128)} %mask_hbm.1), custom_call_target="tpu_custom_call" | custom-call | tf_op jit(solution)/shard_map/exchange/pallas_call | solution.py:303
  107.8 0.0 collective-permute-done.1
  107.9 0.0 collective-permute-done
  107.9 0.0 collective-permute-done.2
  107.9 0.0 collective-permute-done.3
  107.9 0.0 copy-done
  107.9 1.5 fusion.16.field_ref
  109.4 11.7 %gather.1.seen_ref = f32[4,8192]{1,0:T(4,128)} custom-call(f32[4,256,128]{2,1,0:T(8,128)} %fusion.16.field_ref, s32[64,128]{1,0:T(8,128)} %bitcast.18), custom_call_target="tpu_custom_call" | custom-call | tf_op jit(solution)/shard_map/gather/pallas_call | solution.py:346
  121.2 23.2 %finish.1 = (f32[7,8192]{1,0:T(8,128)}, f32[5,256,128]{2,1,0:T(8,128)}) custom-call(s32[128]{0:T(128)} %owner_ref.3, s32[8,128]{1,0:T(8,128)} %get-tuple-element.8.sc_ref, s32[64,128]{1,0:T(8,128)} %get-tuple-element.9.q_ref, s32[64,128]{1,0:T(8,128)} %bitcast.19, f32[128,8,128]{2,1,0:T(8,128)} %exchange.1.ret_ref, f32[4,8192]{1,0:T(4,128)} %gather.1.seen_ref, ...), custom_call_target="tpu_custom_call" | custom-call | tf_op jit(solution)/shard_map/finish/pallas_call | solution.py:421
  144.4 1.4 fusion.21
  145.8 1.3 collective-permute-start.6
  147.1 3.0 %collective-permute-start.7 = (f32[5,32,1,128]{3,2,1,0:T(1,128)S(1)}, f32[5,32,1,128]{3,2,1,0:T(1,128)S(1)}, u32[]{:S(2)}, u32[]{:S(2)}) collective-permute-start(f32[5,32,1,128]{3,2,1,0:T(1,128)S(1)} %get-tuple-element.16), channel_id=1, source_target_pairs={{0,1},{1,2},{2,3},{3,4},{4,5},{5,6},{6,7},{7,8},{8,9},{9,10},{10,1... | collective-permute-start | bytes 245768 | tf_op jit(solution)/shard_map/ppermute | solution.py:446
  150.1 1.5 fusion.22
  151.7 0.3 copy.19
  152.0 1.3 collective-permute-start.5
  153.3 0.3 copy.18
  153.6 5.2 %collective-permute-start.4 = (f32[5,32,8,1]{1,2,3,0:T(8,128)S(1)}, f32[5,32,8,1]{1,2,3,0:T(8,128)S(1)}, u32[]{:S(2)}, u32[]{:S(2)}) collective-permute-start(f32[5,32,8,1]{1,2,3,0:T(8,128)S(1)} %copy.18), channel_id=1, source_target_pairs={{0,32},{32,64},{64,96},{1,33},{33,65},{65,97},{2,34},{34,66},{66,9... | collective-permute-start | bytes 15368 | tf_op jit(solution)/shard_map/ppermute | solution.py:446
  158.8 0.0 collective-permute-done.5
  158.8 0.3 copy.15
  159.2 1.1 collective-permute-done.4
  160.3 0.3 copy.14
  160.6 0.0 collective-permute-done.6
  160.6 0.0 collective-permute-done.7
  160.6 3.9 %fusion.6 = f32[5,32,8,128]{3,2,1,0:T(8,128)S(1)} fusion(f32[5,32,8,128]{3,2,1,0:T(8,128)} %bitcast.13, f32[5,32,8,1]{3,2,1,0:T(8,128)S(1)} %copy.14, f32[5,32,8,1]{3,2,1,0:T(8,128)S(1)} %copy.15, f32[5,32,1,128]{3,2,1,0:T(1,128)S(1)} %collective-permute-done.7, f32[5,32,1,128]{3,2,1,0:T(1,128)S(1)} %collective-permute-done.6), kind=kLoop, calls=%fused_computation.8 | loop fusion | flops 3604480 | bytes 1484800 | tf_op jit(solution)/shard_map/add | solution.py:464
  164.5 0.7 divide_bitcast_fusion
  165.2 0.9 fusion.17
Async XLA Ops:
  0.6 107.3 %copy-start = (f32[4,32,8,128]{3,2,1,0:T(8,128)S(1)}, f32[4,32,8,128]{3,2,1,0:T(8,128)}, u32[]{:S(2)}) copy-start(f32[4,32,8,128]{3,2,1,0:T(8,128)} %param.9) | copy-start | bytes 1572868
  2.0 105.9 %collective-permute-start.2 = (f32[4,32,1,128]{3,2,1,0:T(1,128)S(1)}, f32[4,32,1,128]{3,2,1,0:T(1,128)S(1)}, u32[]{:S(2)}, u32[]{:S(2)}) collective-permute-start(f32[4,32,1,128]{3,2,1,0:T(1,128)S(1)} %get-tuple-element.19), channel_id=1, source_target_pairs={{1,0},{2,1},{3,2},{4,3},{5,4},{6,5},{7,6},{8,7},{9,8},{10,9},{11,1... | collective-permute-start | bytes 196616 | tf_op jit(solution)/shard_map/ppermute | solution.py:447
  3.3 104.6 %collective-permute-start.3 = (f32[4,32,1,128]{3,2,1,0:T(1,128)S(1)}, f32[4,32,1,128]{3,2,1,0:T(1,128)S(1)}, u32[]{:S(2)}, u32[]{:S(2)}) collective-permute-start(f32[4,32,1,128]{3,2,1,0:T(1,128)S(1)} %get-tuple-element.20), channel_id=1, source_target_pairs={{0,1},{1,2},{2,3},{3,4},{4,5},{5,6},{6,7},{7,8},{8,9},{9,10},{10,1... | collective-permute-start | bytes 196616 | tf_op jit(solution)/shard_map/ppermute | solution.py:446
  7.7 100.1 %collective-permute-start.1 = (f32[4,32,8,1]{3,2,1,0:T(8,128)S(1)}, f32[4,32,8,1]{3,2,1,0:T(8,128)S(1)}, u32[]{:S(2)}, u32[]{:S(2)}) collective-permute-start(f32[4,32,8,1]{3,2,1,0:T(8,128)S(1)} %get-tuple-element.21), channel_id=1, source_target_pairs={{32,0},{64,32},{96,64},{33,1},{65,33},{97,65},{34,2},{66,34},{98,6... | collective-permute-start | bytes 12296 | tf_op jit(solution)/shard_map/ppermute | solution.py:447
  9.0 98.8 %collective-permute-start = (f32[4,32,8,1]{3,2,1,0:T(8,128)S(1)}, f32[4,32,8,1]{3,2,1,0:T(8,128)S(1)}, u32[]{:S(2)}, u32[]{:S(2)}) collective-permute-start(f32[4,32,8,1]{3,2,1,0:T(8,128)S(1)} %get-tuple-element.22), channel_id=1, source_target_pairs={{0,32},{32,64},{64,96},{1,33},{33,65},{65,97},{2,34},{34,66},{66,9... | collective-permute-start | bytes 12296 | tf_op jit(solution)/shard_map/ppermute | solution.py:446
  145.8 14.8 %collective-permute-start.6 = (f32[5,32,1,128]{3,2,1,0:T(1,128)S(1)}, f32[5,32,1,128]{3,2,1,0:T(1,128)S(1)}, u32[]{:S(2)}, u32[]{:S(2)}) collective-permute-start(f32[5,32,1,128]{3,2,1,0:T(1,128)S(1)} %get-tuple-element.15), channel_id=1, source_target_pairs={{1,0},{2,1},{3,2},{4,3},{5,4},{6,5},{7,6},{8,7},{9,8},{10,9},{11,1... | collective-permute-start | bytes 245768 | tf_op jit(solution)/shard_map/ppermute | solution.py:447
  147.1 13.5 %collective-permute-start.7 = (f32[5,32,1,128]{3,2,1,0:T(1,128)S(1)}, f32[5,32,1,128]{3,2,1,0:T(1,128)S(1)}, u32[]{:S(2)}, u32[]{:S(2)}) collective-permute-start(f32[5,32,1,128]{3,2,1,0:T(1,128)S(1)} %get-tuple-element.16), channel_id=1, source_target_pairs={{0,1},{1,2},{2,3},{3,4},{4,5},{5,6},{6,7},{7,8},{8,9},{9,10},{10,1... | collective-permute-start | bytes 245768 | tf_op jit(solution)/shard_map/ppermute | solution.py:446
  152.0 6.8 %collective-permute-start.5 = (f32[5,32,8,1]{1,2,3,0:T(8,128)S(1)}, f32[5,32,8,1]{1,2,3,0:T(8,128)S(1)}, u32[]{:S(2)}, u32[]{:S(2)}) collective-permute-start(f32[5,32,8,1]{1,2,3,0:T(8,128)S(1)} %copy.19), channel_id=1, source_target_pairs={{32,0},{64,32},{96,64},{33,1},{65,33},{97,65},{34,2},{66,34},{98,6... | collective-permute-start | bytes 15368 | tf_op jit(solution)/shard_map/ppermute | solution.py:447
  153.6 6.7 %collective-permute-start.4 = (f32[5,32,8,1]{1,2,3,0:T(8,128)S(1)}, f32[5,32,8,1]{1,2,3,0:T(8,128)S(1)}, u32[]{:S(2)}, u32[]{:S(2)}) collective-permute-start(f32[5,32,8,1]{1,2,3,0:T(8,128)S(1)} %copy.18), channel_id=1, source_target_pairs={{0,32},{32,64},{64,96},{1,33},{33,65},{65,97},{2,34},{34,66},{66,9... | collective-permute-start | bytes 15368 | tf_op jit(solution)/shard_map/ppermute | solution.py:446

commit v2 on v1

v2 whole, which is shorter than its diff:
```python
import functools

import jax
import jax.numpy as jnp
from jax import lax
from jax.experimental import pallas as pl
from jax.experimental.pallas import tpu as pltpu
from jax.sharding import PartitionSpec as P

GX_GY = ("gx", "gy")
LOGICAL = pl.DeviceIdType.LOGICAL
F32, BF16, I32 = jnp.float32, jnp.bfloat16, jnp.int32
DEV = 128
PARTS = 8192
PB = 256
NBLK = PARTS // PB
LOG2E = 1.4426950408889634
VMEM = pltpu.VMEM


def iota(shape, dim):
    return lax.broadcasted_iota(I32, shape, dim)


def hot(mask):
    return jnp.where(mask, 1.0, 0.0).astype(BF16)


def split2(x):
    hi = x.astype(BF16)
    lo = (x - hi.astype(F32)).astype(BF16)
    return hi, lo


def dot_nt(a, b):
    return lax.dot_general(a, b, (((1,), (1,)), ((), ())), preferred_element_type=F32)


def dot_nn(a, b):
    return lax.dot_general(a, b, (((1,), (0,)), ((), ())), preferred_element_type=F32)


def dot_tn(a, b):
    return lax.dot_general(a, b, (((0,), (0,)), ((), ())), preferred_element_type=F32)


def row2(ref, k):
    return jnp.concatenate([ref[pl.ds(2 * k, 1), :], ref[pl.ds(2 * k + 1, 1), :]], axis=1)


def add2(ref, x):
    n = x.shape[0]
    ref[0, 0:n] += x[:, :128]
    ref[1, 0:n] += x[:, 128:]


def rank_and_sort(owner_ref, box_ref, pos_ref, mot_ref, rad_ref, tmp_ref, q_ref, sc_ref, rank_ref, acc_ref, sorted_ref, smem_ref, sem):
    tri = hot(iota((PB, PB), 0) < iota((PB, PB), 1))

    def rank_step(k, before):
        box = row2(box_ref, k)
        match = iota((DEV, PB), 0) == box
        within = dot_nn(hot(match), tri)
        rank = jnp.sum(jnp.where(match, within + before, 0.0), axis=0, keepdims=True)
        rank_ref[pl.ds(2 * k, 1), :] = rank[:, :128]
        rank_ref[pl.ds(2 * k + 1, 1), :] = rank[:, 128:]
        return before + jnp.sum(jnp.where(match, 1.0, 0.0), axis=1, keepdims=True)

    counts = lax.fori_loop(0, NBLK, rank_step, jnp.zeros((DEV, 1), F32))
    down, over = iota((DEV, DEV), 0), iota((DEV, DEV), 1)
    wide = jnp.broadcast_to(counts, (DEV, DEV))
    start_row = jnp.sum(jnp.where(down < over, wide, 0.0), axis=0, keepdims=True)
    start_col = jnp.sum(jnp.where(down == over, start_row, 0.0), axis=1, keepdims=True)
    owner_col = jnp.sum(jnp.where(down == over, owner_ref[0:1, :], 0), axis=1, keepdims=True)
    holds = owner_col == over
    start_at = jnp.sum(jnp.where(holds, start_col, 0.0), axis=0, keepdims=True)
    count_at = jnp.sum(jnp.where(holds, counts, 0.0), axis=0, keepdims=True)
    sub = iota((8, DEV), 0)
    sc_ref[...] = jnp.where(sub == 0, start_row, jnp.where(sub == 1, start_at, count_at)).astype(I32)
    copy = pltpu.make_async_copy(sc_ref, smem_ref, sem)
    copy.start()
    table = jnp.broadcast_to(start_row, (64, DEV))
    q = rank_ref[...] + jnp.take_along_axis(table, box_ref[...], axis=1)
    q_ref[...] = q.astype(I32)
    acc_ref[...] = jnp.zeros_like(acc_ref)

    def sort_step(k, carry):
        q = row2(q_ref, k)
        lo_hot = hot(iota((PB, PB), 0) == (q & 255))
        hi_hot = hot(iota((32, PB), 0) == (q >> 8))
        lanes = pl.ds(pl.multiple_of(k * PB, PB), PB)
        rows = [pos_ref[c : c + 1, lanes] for c in range(3)]
        rows += [row2(tmp_ref, k)]
        rows += [mot_ref[c : c + 1, lanes] for c in range(3)]
        rows += [row2(rad_ref, k)]
        rows += [mot_ref[c : c + 1, lanes] for c in range(3, 6)]
        left = spread_rows(rows, hi_hot, 32)
        add2(acc_ref, dot_nt(left, jnp.concatenate([lo_hot, lo_hot], axis=1)))
        return carry

    lax.fori_loop(0, NBLK, sort_step, 0)
    for t in range(64):
        sorted_ref[t, 0:11, :] = acc_ref[t % 2, pl.ds(t // 2, 11, stride=32), :]
    copy.wait()


def spread_rows(rows, hi_hot, n):
    his, los = [], []
    for x in rows:
        hi, lo = split2(jnp.broadcast_to(x, (n, PB)))
        his.append(hi * hi_hot)
        los.append(lo * hi_hot)
    return jnp.concatenate([jnp.concatenate(his, axis=0), jnp.concatenate(los, axis=0)], axis=1)


def windows(sorted_ref, smem_ref, out_ref):
    lane = iota((16, 128), 1)

    def window(o, carry):
        start = smem_ref[1, o]
        count = smem_ref[2, o]
        tile, off = jnp.clip(start >> 7, 0, 64), start & 127
        shift = (128 - off) & 127
        low = pltpu.roll(sorted_ref[tile], shift, 1)
        high = pltpu.roll(sorted_ref[tile + 1], shift, 1)
        both = jnp.where(lane < 128 - off, low, high)
        out_ref[o] = jnp.where(lane < count, both, 0.0)
        return carry

    lax.fori_loop(0, DEV, window, 0, unroll=8)


def contact_block(s, mask):
    sub = iota((8, 128), 0)
    top = s[0:8]
    r = s[7:8]
    occupied = jnp.where(r > 0.0, 1.0, 0.0)
    scale = jnp.where((sub & 3) == 3, 1.4142135623730951, (2.0 * LOG2E) ** 0.5)
    pos4 = jnp.concatenate([s[0:3], r, s[0:3], r], axis=0)
    y = pos4 * scale
    a = y.astype(BF16).astype(F32)
    b = (y - a).astype(BF16).astype(F32)
    c = y - a - b
    first = sub < 4
    is_r = (sub & 3) == 3
    sq = y * y * 0.5
    m = jnp.sum(jnp.where(first & ~is_r, sq, 0.0), axis=0, keepdims=True)
    g = sq[3:4] + 0.5

    def three(v):
        v1 = v.astype(BF16).astype(F32)
        v2 = (v - v1).astype(BF16).astype(F32)
        return v1, v2, v - v1 - v2

    m1, m2, m3 = three(m)
    g1, g2, g3 = three(g)

    def pick(rows):
        out = jnp.zeros((8, 128), F32)
        for i, v in enumerate(rows):
            out = jnp.where(sub == i, v, out)
        return out

    zero = jnp.zeros((8, 128), F32)
    left = jnp.concatenate(
        [a, b, jnp.where(first, a, c), pick([m1, m2, m3, 1.0, 1.0, 1.0]), pick([g1, g2, g3, 1.0, 1.0, 1.0]), zero], axis=0
    ).astype(BF16)
    h1 = jnp.where(first, a, b)
    h3 = jnp.where(first, c, a)
    h4 = pick([-1.0, -1.0, -1.0, -m1, -m2, -m3])
    h5 = pick([1.0, 1.0, 1.0, g1, g2, g3])
    e_cols = jnp.concatenate(
        [jnp.where(is_r, 0.0, h1), jnp.where(is_r, 0.0, h1), jnp.where(is_r, 0.0, h3), h4, zero, zero], axis=0
    )
    r_cols = jnp.concatenate(
        [jnp.where(is_r, h1, 0.0), jnp.where(is_r, h1, 0.0), jnp.where(is_r, h3, 0.0), zero, h5, zero], axis=0
    )
    right = jnp.concatenate([e_cols, r_cols], axis=1).astype(BF16)
    pair = dot_tn(left, right)
    weight = jnp.where(mask != 0, jnp.exp2(pair[:, :128] / pair[:, 128:]), 0.0)
    wh, wl = split2(weight)
    top_o = jnp.where(sub == 7, occupied, top)
    stacked = jnp.concatenate([top_o, s[8:16]], axis=0)
    sh, sl = split2(stacked)
    lhs = jnp.concatenate(
        [jnp.concatenate([sh, sh], axis=1), jnp.concatenate([sl, jnp.zeros_like(sl)], axis=1)], axis=0
    )
    mixed = dot_nt(lhs, jnp.concatenate([wh, wl], axis=1))
    mixed = mixed[0:16] + mixed[16:32]
    ws = mixed[7:8]
    diff = top * ws - mixed[0:8]
    c1 = jnp.where(sub == 3, -0.03, 0.05)
    c2 = jnp.where(sub == 3, 0.0, 0.02)
    spin = s[8:16] - 0.01 * (s[8:16] * ws + mixed[8:16])
    return jnp.where(first, c1 * diff - c2 * pltpu.roll(diff, 4, 0), pltpu.roll(spin, 4, 0))


def edges(src_ref, n, ylow_ref, yhigh_ref, xlow_ref, xhigh_ref):
    lane = iota((8, 128), 1)
    first = jnp.zeros((8, 128), F32)
    last = jnp.zeros((8, 128), F32)
    for j in range(n * 32):
        v = src_ref[8 * j : 8 * j + 8, :]
        ylow_ref[j : j + 1, :] = v[0:1]
        yhigh_ref[j : j + 1, :] = v[7:8]
        first = jnp.where(lane == j, pltpu.roll(v, j, 1), first)
        last = jnp.where(lane == j, pltpu.roll(v, (j + 1) % 128, 1), last)
    xlow_ref[...] = first
    xhigh_ref[...] = last


def neighbours():
    ix, iy = lax.axis_index("gx"), lax.axis_index("gy")
    up_x = lax.rem(ix + 1, 4) * 32 + iy
    down_x = lax.rem(ix + 3, 4) * 32 + iy
    up_y = ix * 32 + lax.rem(iy + 1, 32)
    down_y = ix * 32 + lax.rem(iy + 31, 32)
    return down_y, up_y, down_x, up_x


def halo_copies(mine, theirs, send_sem, recv_sem):
    down_y, up_y, down_x, up_x = neighbours()
    plan = ((0, 1, down_y), (1, 0, up_y), (2, 3, down_x), (3, 2, up_x))
    return [
        pltpu.make_async_remote_copy(
            mine[a], theirs[b], send_sem.at[a], recv_sem.at[b], device_id=dev, device_id_type=LOGICAL
        )
        for a, b, dev in plan
    ]


def smooth(src_ref, n, halo, out_ref):
    ylo, yhi, xlo_ref, xhi_ref = halo
    ix, iy = lax.axis_index("gx"), lax.axis_index("gy")
    sub, lane = iota((8, 128), 0), iota((8, 128), 1)
    xlo = jnp.where(ix > 0, xlo_ref[...], 0.0)
    xhi = jnp.where(ix < 3, xhi_ref[...], 0.0)
    zero = jnp.zeros((8, 128), F32)
    for f in range(n):
        for z in range(32):
            j = f * 32 + z
            at = lambda i: src_ref[8 * i : 8 * i + 8, :]
            c = at(j)
            total = (at(j - 1) if z > 0 else zero) + (at(j + 1) if z < 31 else zero)
            low = jnp.where(iy > 0, ylo[j : j + 1, :], 0.0)
            high = jnp.where(iy < 31, yhi[j : j + 1, :], 0.0)
            total += jnp.where(sub == 0, low, pltpu.roll(c, 1, 0))
            total += jnp.where(sub == 7, high, pltpu.roll(c, 7, 0))
            total += jnp.where(lane == 0, pltpu.roll(xlo, (128 - j) % 128, 1), pltpu.roll(c, 1, 1))
            total += jnp.where(lane == 127, pltpu.roll(xhi, (255 - j) % 128, 1), pltpu.roll(c, 127, 1))
            out_ref[8 * j : 8 * j + 8, :] = 0.25 * c + 0.125 * total


def gather(field_ref, cell_ref, seen_ref, f_ref):
    for c in range(4):
        hi, lo = split2(jnp.transpose(field_ref[256 * c : 256 * c + 256, :]))
        f_ref[pl.ds(128 * c, 128), 0:256] = hi
        f_ref[pl.ds(128 * c, 128), 256:512] = lo

    def step(k, carry):
        cell = row2(cell_ref, k)
        high = hot(iota((256, PB), 0) == (cell >> 7))
        part = dot_nn(f_ref[...], jnp.concatenate([high, high], axis=0))
        low = iota((128, PB), 0) == (cell & 127)
        rows = [
            jnp.sum(jnp.where(low, part[128 * c : 128 * c + 128], 0.0), axis=0, keepdims=True)
            for c in range(4)
        ]
        seen_ref[:, pl.ds(pl.multiple_of(k * PB, PB), PB)] = jnp.concatenate(rows, axis=0)
        return carry

    lax.fori_loop(0, NBLK, step, 0)


def deposit_block(rows, cell, acc_ref):
    lo_hot = hot(iota((256, PB), 0) == (cell & 255))
    hi_hot = hot(iota((128, PB), 0) == (cell >> 8))
    left = spread_rows(rows, hi_hot, 128)
    add2(acc_ref, dot_nt(left, jnp.concatenate([lo_hot, lo_hot], axis=1)))


def unfold(acc_ref, n, dep_ref):
    for j in range(2):
        dep_ref[pl.ds(j, n * 128, stride=2), :] = acc_ref[j]


def drag_of(seen_ref, mot_ref, r, lanes):
    return 4.0 / (r * r + 0.25) * (seen_ref[0:3, lanes] - mot_ref[0:3, lanes])


GROUP = 8


def main_kernel(
    owner_ref, box_ref, pos_ref, mot_ref, rad_ref, tmp_ref, cell_ref, fluid_ref, mask_hbm,
    ret_ref, q_ref, sc_ref, seen_ref, spread_ref,
    rank_ref, acc_ref, sorted_ref, smem_ref, out_ref, got_ref, res_ref, mask_ref,
    field_ref, f_ref, dacc_ref, dep_ref,
    ey0, ey1, ex0, ex1, hy0, hy1, hx0, hx1,
    gy0, gy1, gx0, gx1, ky0, ky1, kx0, kx1,
    table_sem, send_sem, got_sem, back_sem, ret_sem, mask_sem, hs_sem, hr_sem, ks_sem, kr_sem,
):
    me = lax.axis_index("gx") * 32 + lax.axis_index("gy")
    got_ref[...] = jnp.zeros_like(got_ref)
    barrier = pltpu.get_barrier_semaphore()

    def signal(d, carry):
        pl.semaphore_signal(barrier, inc=1, device_id=lax.rem(me + d, DEV), device_id_type=LOGICAL)
        return carry

    lax.fori_loop(1, DEV, signal, 0)

    def mask_copy(i):
        part = pl.ds(16 * i, 16)
        return pltpu.make_async_copy(mask_hbm.at[part], mask_ref.at[part], mask_sem.at[i])

    for i in range(8):
        mask_copy(i).start()
    edges(fluid_ref, 4, ey0, ey1, ex0, ex1)
    rank_and_sort(owner_ref, box_ref, pos_ref, mot_ref, rad_ref, tmp_ref, q_ref, sc_ref, rank_ref, acc_ref, sorted_ref, smem_ref, table_sem)
    windows(sorted_ref, smem_ref, out_ref)
    pl.semaphore_wait(barrier, DEV - 1)
    fluid_halo = halo_copies((ey0, ey1, ex0, ex1), (hy0, hy1, hx0, hx1), hs_sem, hr_sem)
    for copy in fluid_halo:
        copy.start()

    def send(d):
        peer = lax.rem(me + d, DEV)
        return pltpu.make_async_remote_copy(
            out_ref.at[peer, pl.ds(0, 11)], got_ref.at[me, pl.ds(0, 11)],
            send_sem.at[d], got_sem.at[me], device_id=peer, device_id_type=LOGICAL,
        )

    def got(d):
        peer = lax.rem(me + DEV - d, DEV)
        return pltpu.make_async_remote_copy(
            out_ref.at[peer, pl.ds(0, 11)], got_ref.at[peer, pl.ds(0, 11)],
            send_sem.at[d], got_sem.at[peer], device_id=peer, device_id_type=LOGICAL,
        )

    def back(d):
        peer = lax.rem(me + DEV - d, DEV)
        return pltpu.make_async_remote_copy(
            res_ref.at[peer, pl.ds(0, 7)], ret_ref.at[me, pl.ds(0, 7)],
            back_sem.at[d], ret_sem.at[me], device_id=peer, device_id_type=LOGICAL,
        )

    def returned(d):
        peer = lax.rem(me + d, DEV)
        return pltpu.make_async_remote_copy(
            res_ref.at[peer, pl.ds(0, 7)], ret_ref.at[peer, pl.ds(0, 7)],
            back_sem.at[d], ret_sem.at[peer], device_id=peer, device_id_type=LOGICAL,
        )

    def start_send(d, carry):
        send(d).start()
        return carry

    lax.fori_loop(1, DEV, start_send, 0)
    got_ref[me] = out_ref[me]
    for copy in fluid_halo:
        copy.wait()
    smooth(fluid_ref, 4, (hy0, hy1, hx0, hx1), field_ref)
    gather(field_ref, cell_ref, seen_ref, f_ref)
    for i in range(8):
        mask_copy(i).wait()

    def contacts(first):
        peers = [lax.rem(me + DEV - (first + k), DEV) for k in range(GROUP)]
        given = [got_ref[p] for p in peers]
        results = [contact_block(s, mask_ref[p]) for s, p in zip(given, peers)]
        for p, r in zip(peers, results):
            res_ref[p] = r

    def await_group(first, skip):
        for k in range(skip, GROUP):
            got(first + k).wait_recv()

    def send_back(first, skip):
        for k in range(skip, GROUP):
            back(first + k).start()

    await_group(0, 1)
    contacts(0)
    await_group(GROUP, 0)
    contacts(GROUP)
    send_back(0, 1)

    def group(g, carry):
        await_group(g * GROUP, 0)
        contacts(g * GROUP)
        send_back(g * GROUP - GROUP, 0)
        return carry

    lax.fori_loop(2, DEV // GROUP, group, 0)
    for k in range(GROUP):
        back(DEV - GROUP + k).start()
    ret_ref[me] = res_ref[me]

    dacc_ref[...] = jnp.zeros_like(dacc_ref)

    def deposit(k, carry):
        lanes = pl.ds(pl.multiple_of(k * PB, PB), PB)
        r = row2(rad_ref, k)
        volume = r * r * r
        push = -volume * drag_of(seen_ref, mot_ref, r, lanes)
        deposit_block([volume, push[0:1], push[1:2], push[2:3]], row2(cell_ref, k), dacc_ref)
        return carry

    lax.fori_loop(0, NBLK, deposit, 0)
    unfold(dacc_ref, 4, dep_ref)
    edges(dep_ref, 4, gy0, gy1, gx0, gx1)
    dep_halo = halo_copies((gy0, gy1, gx0, gx1), (ky0, ky1, kx0, kx1), ks_sem, kr_sem)
    for copy in dep_halo:
        copy.start()

    def close(d, carry):
        send(d).wait_send()
        back(d).wait_send()
        returned(d).wait_recv()
        return carry

    lax.fori_loop(1, DEV, close, 0)
    for copy in dep_halo:
        copy.wait()
    smooth(dep_ref, 4, (ky0, ky1, kx0, kx1), spread_ref)


def halo_scratch(n):
    return [VMEM((n * 32, 128), F32), VMEM((n * 32, 128), F32), VMEM((8, 128), F32), VMEM((8, 128), F32)]


def vmem_specs(n):
    return [pl.BlockSpec(memory_space=VMEM)] * n


def main(owner, box, pos, mot, rad, tmp, cell, fluid, mask):
    dma = pltpu.SemaphoreType.DMA
    return pl.pallas_call(
        main_kernel,
        out_shape=(
            jax.ShapeDtypeStruct((DEV, 8, 128), F32),
            jax.ShapeDtypeStruct((64, 128), I32),
            jax.ShapeDtypeStruct((8, 128), I32),
            jax.ShapeDtypeStruct((4, PARTS), F32),
            jax.ShapeDtypeStruct((1024, 128), F32),
        ),
        in_specs=vmem_specs(8) + [pl.BlockSpec(memory_space=pl.ANY)],
        out_specs=tuple(vmem_specs(5)),
        scratch_shapes=[
            VMEM((64, 128), F32),
            VMEM((2, 384, 128), F32),
            VMEM((66, 16, 128), F32),
            pltpu.SMEM((8, 128), I32),
            VMEM((DEV, 16, 128), F32),
            VMEM((DEV, 16, 128), F32),
            VMEM((DEV, 8, 128), F32),
            VMEM((DEV, 128, 128), I32),
            VMEM((1024, 128), F32),
            VMEM((512, 512), BF16),
            VMEM((2, 512, 128), F32),
            VMEM((1032, 128), F32),
            *halo_scratch(4), *halo_scratch(4), *halo_scratch(4), *halo_scratch(4),
            dma, dma((DEV,)), dma((DEV,)), dma((DEV,)), dma((DEV,)), dma((8,)),
            dma((4,)), dma((4,)), dma((4,)), dma((4,)),
        ],
        compiler_params=pltpu.CompilerParams(collective_id=0, has_side_effects=True),
        name="main",
    )(owner, box, pos, mot, rad, tmp, cell, fluid, mask)


def fetch_kernel(
    owner_ref, sc_ref, q_ref, cell_ref, ret_ref, seen_ref, mot_ref, rad_ref, tmp_ref,
    next_ref, dep_ref,
    dense_ref, left_ref, acc_ref,
):
    lane = iota((8, 128), 1)

    def pack(b, carry):
        start = sc_ref[0, b]
        tile, off = jnp.clip(start >> 7, 0, 64), start & 127
        mine = pltpu.roll(ret_ref[owner_ref[b]], off, 1)
        dense_ref[tile] = jnp.where(lane < off, dense_ref[tile], mine)
        dense_ref[tile + 1] = mine
        return carry

    lax.fori_loop(0, DEV, pack, 0, unroll=2)
    hi, lo = split2(dense_ref[0:64].reshape(512, 128))
    left_ref[:, 0:128] = hi
    left_ref[:, 128:256] = lo
    acc_ref[...] = jnp.zeros_like(acc_ref)

    def step(k, carry):
        lanes = pl.ds(pl.multiple_of(k * PB, PB), PB)
        q = row2(q_ref, k)
        low = hot(iota((128, PB), 0) == (q & 127))
        part = dot_nn(left_ref[...], jnp.concatenate([low, low], axis=0))
        high = jnp.broadcast_to(q >> 7, (8, PB))
        res = part[0:8]
        for t in range(1, 64):
            res = jnp.where(high == t, part[8 * t : 8 * t + 8], res)
        r = row2(rad_ref, k)
        temp = row2(tmp_ref, k)
        gas = seen_ref[3:4, lanes]
        drag = drag_of(seen_ref, mot_ref, r, lanes)
        vn = mot_ref[0:3, lanes] + (res[0:3] + 0.1 * drag) - jnp.where(iota((3, PB), 0) == 2, 0.03, 0.0)
        tn = temp + (res[3:4] + 0.4 * (gas - temp))
        next_ref[0:3, lanes] = vn
        next_ref[3:6, lanes] = res[4:7]
        next_ref[6:7, lanes] = tn
        deposit_block([r * r * r * (tn - gas)], row2(cell_ref, k), acc_ref)
        return carry

    lax.fori_loop(0, NBLK, step, 0)
    unfold(acc_ref, 1, dep_ref)


def fetch(owner, sc, q, cell, ret, seen, mot, rad, tmp):
    return pl.pallas_call(
        fetch_kernel,
        out_shape=(jax.ShapeDtypeStruct((7, PARTS), F32), jax.ShapeDtypeStruct((264, 128), F32)),
        in_specs=[pl.BlockSpec(memory_space=pltpu.SMEM)] * 2 + vmem_specs(7),
        out_specs=tuple(vmem_specs(2)),
        scratch_shapes=[VMEM((66, 8, 128), F32), VMEM((512, 256), BF16), VMEM((2, 128, 128), F32)],
        name="fetch",
    )(owner, sc, q, cell, ret, seen, mot, rad, tmp)


def end_kernel(
    dep_ref, spread_ref, fluid_ref, next_ref, void_ref,
    heat_ref, ey0, ey1, ex0, ex1, hy0, hy1, hx0, hx1, hs_sem, hr_sem,
):
    barrier = pltpu.get_barrier_semaphore()
    for dev in neighbours():
        pl.semaphore_signal(barrier, inc=1, device_id=dev, device_id_type=LOGICAL)
    edges(dep_ref, 1, ey0, ey1, ex0, ex1)
    crowding = 1.0 + 4.0 * spread_ref[0:256, :]
    void_ref[...] = 1.0 / crowding
    scale = 0.4 * crowding
    pl.semaphore_wait(barrier, 4)
    halo = halo_copies((ey0, ey1, ex0, ex1), (hy0, hy1, hx0, hx1), hs_sem, hr_sem)
    for copy in halo:
        copy.start()
    for f in range(3):
        at = slice(256 * f, 256 * f + 256)
        next_ref[at, :] = fluid_ref[at, :] + spread_ref[256 * f + 256 : 256 * f + 512, :] * scale
    for copy in halo:
        copy.wait()
    smooth(dep_ref, 1, (hy0, hy1, hx0, hx1), heat_ref)
    next_ref[768:1024, :] = fluid_ref[768:1024, :] + heat_ref[...] * scale


def end(dep, spread, fluid):
    dma = pltpu.SemaphoreType.DMA
    return pl.pallas_call(
        end_kernel,
        out_shape=(jax.ShapeDtypeStruct((1024, 128), F32), jax.ShapeDtypeStruct((256, 128), F32)),
        in_specs=vmem_specs(3),
        out_specs=tuple(vmem_specs(2)),
        scratch_shapes=[VMEM((256, 128), F32), *halo_scratch(1), *halo_scratch(1), dma((4,)), dma((4,))],
        compiler_params=pltpu.CompilerParams(collective_id=1, has_side_effects=True),
        name="end",
    )(dep, spread, fluid)


def shards(fluid, pos, mot, rad, tmp, cell, box, box_owner, mask):
    rad2, tmp2 = rad.reshape(64, 128), tmp.reshape(64, 128)
    cell2, box2 = cell.reshape(64, 128), box.reshape(64, 128)
    fluid2 = fluid.reshape(1024, 128)
    ret, q, sc, seen, spread = main(box_owner.reshape(1, 128), box2, pos, mot, rad2, tmp2, cell2, fluid2, mask)
    nxt, dep = fetch(box_owner, sc, q, cell2, ret, seen, mot, rad2, tmp2)
    fluid_next, void = end(dep, spread, fluid2)
    return fluid_next.reshape(4, 32, 8, 128), void.reshape(32, 8, 128), nxt


def solution(mesh):
    return jax.shard_map(
        shards,
        mesh=mesh,
        in_specs=(
            P(None, None, "gy", "gx"),
            P(None, GX_GY),
            P(None, GX_GY),
            P(GX_GY),
            P(GX_GY),
            P(GX_GY),
            P(GX_GY, None),
            P(),
            P(GX_GY, None, None),
        ),
        out_specs=(P(None, None, "gy", "gx"), P(None, "gy", "gx"), P(None, GX_GY)),
        check_vma=False,
    )
```

time: 168 us -> 111 us (0.66); the launches traced: 166 us -> 111 us
  Pallas kernels: 129 us -> 107 us
  starting transfers between devices: 21 us -> 0 us
  other arithmetic: 6.96 us -> 0 us
  local copies, waits for them, and re-layouts: 7.01 us -> 3.44 us
    pallas_call x4 -> x3, Pallas kernels: 129 us -> 107 us  [the longest x1 73.5 us: main(): pl.pallas_call(main_kernel, out_shape=(jax.ShapeDtypeStruct((DEV, 8, 128)...]
    ppermute x8 -> x0, starting transfers between devices: 21 us -> none  [the longest x4 15.9 us: with_halo(): lax.ppermute(last, axis, up)]
    slice x4 -> x0, local copies, waits for them, and re-layouts: 5.69 us -> none  [with_halo(): first = lax.slice_in_dim(value, 0, 1, axis=dim)]
    add x2 -> x0, other arithmetic: 4.73 us -> none  [the longest x1 3.88 us: stencil(): return 0.25 * interior + 0.125 * beside_all]
    unnamed x4 -> x2, local copies, waits for them, and re-layouts: 0.65 us -> 3.44 us
  transfers between devices with their start and end apart: 8 -> 0, of which waited for: 1 -> 0; matrix products, arithmetic and copies ran while one was open for 3% -> 0% of each run, Pallas kernels for 57% -> 0%
where the time goes in v2:
time: 111 us
  Pallas kernels  107 us (96%)
  local copies, waits for them, and re-layouts  3.44 us (3%)
    pallas_call x1, Pallas kernels, main(): pl.pallas_call(main_kernel, out_shape=(jax.ShapeDtypeStruct((DEV, 8, 128)...  73.5 us
    pallas_call x1, Pallas kernels, fetch(): pl.pallas_call(fetch_kernel, out_shape=(jax.ShapeDtypeStruct((7, PARTS),...  23.3 us
    pallas_call x1, Pallas kernels, end(): pl.pallas_call(end_kernel, out_shape=(jax.ShapeDtypeStruct((1024, 128), F...  9.93 us
    unnamed x2, local copies, waits for them, and re-layouts  3.44 us

profile of v2, /device:TPU:0, one launch (start us, length us, event | category | flops | bytes accessed | tf_op | source)
XLA Modules:
  0.0 110.8 jit_solution(8427341411374727714)
XLA Ops:
  0.6 73.5 %main.1 = (f32[128,8,128]{2,1,0:T(8,128)}, s32[64,128]{1,0:T(8,128)}, s32[8,128]{1,0:T(8,128)}, f32[4,8192]{1,0:T(4,128)}, f32[1024,128]{1,0:T(8,128)}) custom-call(s32[1,128]{1,0:T(1,128)} %bitcast.19, s32[64,128]{1,0:T(8,128)} %bitcast.18, f32[3,8192]{1,0:T(4,128)} %pos_ref.1, f32[6,8192]{1,0:T(8,128)} %mot_ref.3, f32[64,128]{1,0:T(8,128)} %bitcast.11, ...), custom_call_target="tpu_custom_call" | custom-call | tf_op jit(solution)/shard_map/main/pallas_call | solution.py:439
  74.1 23.3 %fetch.1 = (f32[7,8192]{1,0:T(8,128)}, f32[264,128]{1,0:T(8,128)}) custom-call(s32[128]{0:T(128)} %owner_ref.1, s32[8,128]{1,0:T(8,128)} %get-tuple-element.12.sc_ref, s32[64,128]{1,0:T(8,128)} %get-tuple-element.13.q_ref, s32[64,128]{1,0:T(8,128)} %bitcast.16, f32[128,8,128]{2,1,0:T(8,128)} %get-tuple-element.14.ret_ref, ...), custom_call_target="tpu_custom_call" | custom-call | tf_op jit(solution)/shard_map/fetch/pallas_call | solution.py:519
  97.4 9.9 %end.1 = (f32[1024,128]{1,0:T(8,128)}, f32[256,128]{1,0:T(8,128)}) custom-call(f32[264,128]{1,0:T(8,128)} %get-tuple-element.16.dep_ref, f32[1024,128]{1,0:T(8,128)} %get-tuple-element.17.spread_ref, f32[1024,128]{1,0:T(8,128)} %bitcast.9), custom_call_target="tpu_custom_call" | custom-call | tf_op jit(solution)/shard_map/end/pallas_call | solution.py:555
  107.4 1.9 %copy.14 = f32[4,32,8,128]{3,2,1,0:T(8,128)} copy(f32[4,32,8,128]{3,2,1,0:T(8,128)} %bitcast.10) | data formatting | bytes 1048576
  109.2 1.6 %copy.15 = f32[32,8,128]{2,1,0:T(8,128)} copy(f32[32,8,128]{2,1,0:T(8,128)} %bitcast.17) | data formatting | bytes 262144

commit v3 on v2

--- a/solution.py
+++ b/solution.py
@@ -12,7 +12,8 @@
 F32, BF16, I32 = jnp.float32, jnp.bfloat16, jnp.int32
 DEV = 128
 PARTS = 8192
-PB = 256
+RB = 256
+PB = 2048
 NBLK = PARTS // PB
 LOG2E = 1.4426950408889634
 VMEM = pltpu.VMEM
@@ -44,29 +45,32 @@
     return lax.dot_general(a, b, (((0,), (0,)), ((), ())), preferred_element_type=F32)
 
 
-def row2(ref, k):
-    return jnp.concatenate([ref[pl.ds(2 * k, 1), :], ref[pl.ds(2 * k + 1, 1), :]], axis=1)
+def row2(ref, k, size=PB):
+    n = size // 128
+    return jnp.concatenate([ref[pl.ds(n * k + i, 1), :] for i in range(n)], axis=1)
 
 
 def add2(ref, x):
-    n = x.shape[0]
+    n = x.shape[0] // 2
+    x = x[:n] + x[n:]
     ref[0, 0:n] += x[:, :128]
     ref[1, 0:n] += x[:, 128:]
 
 
-def rank_and_sort(owner_ref, box_ref, pos_ref, mot_ref, rad_ref, tmp_ref, q_ref, sc_ref, rank_ref, acc_ref, sorted_ref, smem_ref, sem):
-    tri = hot(iota((PB, PB), 0) < iota((PB, PB), 1))
+def rank_and_sort(signal, owner_ref, box_ref, pos_ref, mot_ref, rad_ref, tmp_ref, q_ref, sc_ref, rank_ref, acc_ref, sorted_ref, smem_ref, sem):
+    tri = hot(iota((RB, RB), 0) < iota((RB, RB), 1))
 
     def rank_step(k, before):
-        box = row2(box_ref, k)
-        match = iota((DEV, PB), 0) == box
+        signal(k)
+        box = row2(box_ref, k, RB)
+        match = iota((DEV, RB), 0) == box
         within = dot_nn(hot(match), tri)
         rank = jnp.sum(jnp.where(match, within + before, 0.0), axis=0, keepdims=True)
         rank_ref[pl.ds(2 * k, 1), :] = rank[:, :128]
         rank_ref[pl.ds(2 * k + 1, 1), :] = rank[:, 128:]
         return before + jnp.sum(jnp.where(match, 1.0, 0.0), axis=1, keepdims=True)
 
-    counts = lax.fori_loop(0, NBLK, rank_step, jnp.zeros((DEV, 1), F32))
+    counts = lax.fori_loop(0, PARTS // RB, rank_step, jnp.zeros((DEV, 1), F32), unroll=8)
     down, over = iota((DEV, DEV), 0), iota((DEV, DEV), 1)
     wide = jnp.broadcast_to(counts, (DEV, DEV))
     start_row = jnp.sum(jnp.where(down < over, wide, 0.0), axis=0, keepdims=True)
@@ -86,7 +90,7 @@
 
     def sort_step(k, carry):
         q = row2(q_ref, k)
-        lo_hot = hot(iota((PB, PB), 0) == (q & 255))
+        lo_hot = hot(iota((256, PB), 0) == (q & 255))
         hi_hot = hot(iota((32, PB), 0) == (q >> 8))
         lanes = pl.ds(pl.multiple_of(k * PB, PB), PB)
         rows = [pos_ref[c : c + 1, lanes] for c in range(3)]
@@ -95,7 +99,7 @@
         rows += [row2(rad_ref, k)]
         rows += [mot_ref[c : c + 1, lanes] for c in range(3, 6)]
         left = spread_rows(rows, hi_hot, 32)
-        add2(acc_ref, dot_nt(left, jnp.concatenate([lo_hot, lo_hot], axis=1)))
+        add2(acc_ref, dot_nt(left, lo_hot))
         return carry
 
     lax.fori_loop(0, NBLK, sort_step, 0)
@@ -110,24 +114,19 @@
         hi, lo = split2(jnp.broadcast_to(x, (n, PB)))
         his.append(hi * hi_hot)
         los.append(lo * hi_hot)
-    return jnp.concatenate([jnp.concatenate(his, axis=0), jnp.concatenate(los, axis=0)], axis=1)
-
-
-def windows(sorted_ref, smem_ref, out_ref):
+    return jnp.concatenate(his + los, axis=0)
+
+
+def window(sorted_ref, smem_ref, o):
     lane = iota((16, 128), 1)
-
-    def window(o, carry):
-        start = smem_ref[1, o]
-        count = smem_ref[2, o]
-        tile, off = jnp.clip(start >> 7, 0, 64), start & 127
-        shift = (128 - off) & 127
-        low = pltpu.roll(sorted_ref[tile], shift, 1)
-        high = pltpu.roll(sorted_ref[tile + 1], shift, 1)
-        both = jnp.where(lane < 128 - off, low, high)
-        out_ref[o] = jnp.where(lane < count, both, 0.0)
-        return carry
-
-    lax.fori_loop(0, DEV, window, 0, unroll=8)
+    start = smem_ref[1, o]
+    count = smem_ref[2, o]
+    tile, off = jnp.clip(start >> 7, 0, 64), start & 127
+    shift = (128 - off) & 127
+    low = pltpu.roll(sorted_ref[tile], shift, 1)
+    high = pltpu.roll(sorted_ref[tile + 1], shift, 1)
+    both = jnp.where(lane < 128 - off, low, high)
+    return jnp.where(lane < count, both, 0.0)
 
 
 def contact_block(s, mask):
@@ -254,13 +253,14 @@
 def gather(field_ref, cell_ref, seen_ref, f_ref):
     for c in range(4):
         hi, lo = split2(jnp.transpose(field_ref[256 * c : 256 * c + 256, :]))
-        f_ref[pl.ds(128 * c, 128), 0:256] = hi
-        f_ref[pl.ds(128 * c, 128), 256:512] = lo
+        f_ref[pl.ds(128 * c, 128), :] = hi
+        f_ref[pl.ds(512 + 128 * c, 128), :] = lo
 
     def step(k, carry):
         cell = row2(cell_ref, k)
         high = hot(iota((256, PB), 0) == (cell >> 7))
-        part = dot_nn(f_ref[...], jnp.concatenate([high, high], axis=0))
+        part = dot_nn(f_ref[...], high)
+        part = part[:512] + part[512:]
         low = iota((128, PB), 0) == (cell & 127)
         rows = [
             jnp.sum(jnp.where(low, part[128 * c : 128 * c + 128], 0.0), axis=0, keepdims=True)
@@ -276,7 +276,7 @@
     lo_hot = hot(iota((256, PB), 0) == (cell & 255))
     hi_hot = hot(iota((128, PB), 0) == (cell >> 8))
     left = spread_rows(rows, hi_hot, 128)
-    add2(acc_ref, dot_nt(left, jnp.concatenate([lo_hot, lo_hot], axis=1)))
+    add2(acc_ref, dot_nt(left, lo_hot))
 
 
 def unfold(acc_ref, n, dep_ref):
@@ -286,6 +286,20 @@
 
 def drag_of(seen_ref, mot_ref, r, lanes):
     return 4.0 / (r * r + 0.25) * (seen_ref[0:3, lanes] - mot_ref[0:3, lanes])
+
+
+def deposit_four(seen_ref, mot_ref, rad_ref, cell_ref, acc_ref):
+    acc_ref[...] = jnp.zeros_like(acc_ref)
+
+    def step(k, carry):
+        lanes = pl.ds(pl.multiple_of(k * PB, PB), PB)
+        r = row2(rad_ref, k)
+        volume = r * r * r
+        push = -volume * drag_of(seen_ref, mot_ref, r, lanes)
+        deposit_block([volume, push[0:1], push[1:2], push[2:3]], row2(cell_ref, k), acc_ref)
+        return carry
+
+    lax.fori_loop(0, NBLK, step, 0)
 
 
 GROUP = 8
@@ -304,11 +318,17 @@
     got_ref[...] = jnp.zeros_like(got_ref)
     barrier = pltpu.get_barrier_semaphore()
 
-    def signal(d, carry):
-        pl.semaphore_signal(barrier, inc=1, device_id=lax.rem(me + d, DEV), device_id_type=LOGICAL)
-        return carry
-
-    lax.fori_loop(1, DEV, signal, 0)
+    def signal(k):
+        for i in range(4):
+            d = 4 * k + i + 1
+
+            def one():
+                pl.semaphore_signal(barrier, inc=1, device_id=lax.rem(me + d, DEV), device_id_type=LOGICAL)
+
+            if i < 3:
+                one()
+            else:
+                pl.when(d < DEV)(one)
 
     def mask_copy(i):
         part = pl.ds(16 * i, 16)
@@ -317,8 +337,7 @@
     for i in range(8):
         mask_copy(i).start()
     edges(fluid_ref, 4, ey0, ey1, ex0, ex1)
-    rank_and_sort(owner_ref, box_ref, pos_ref, mot_ref, rad_ref, tmp_ref, q_ref, sc_ref, rank_ref, acc_ref, sorted_ref, smem_ref, table_sem)
-    windows(sorted_ref, smem_ref, out_ref)
+    rank_and_sort(signal, owner_ref, box_ref, pos_ref, mot_ref, rad_ref, tmp_ref, q_ref, sc_ref, rank_ref, acc_ref, sorted_ref, smem_ref, table_sem)
     pl.semaphore_wait(barrier, DEV - 1)
     fluid_halo = halo_copies((ey0, ey1, ex0, ex1), (hy0, hy1, hx0, hx1), hs_sem, hr_sem)
     for copy in fluid_halo:
@@ -352,12 +371,28 @@
             back_sem.at[d], ret_sem.at[peer], device_id=peer, device_id_type=LOGICAL,
         )
 
-    def start_send(d, carry):
-        send(d).start()
+    def fill(first):
+        peers = [lax.rem(me + first + k, DEV) for k in range(GROUP)]
+        rows = [window(sorted_ref, smem_ref, p) for p in peers]
+        for p, r in zip(peers, rows):
+            out_ref[p] = r
+
+    def send_group(first, skip):
+        for k in range(skip, GROUP):
+            send(first + k).start()
+
+    fill(0)
+    got_ref[me] = out_ref[me]
+    fill(GROUP)
+    send_group(0, 1)
+
+    def fill_and_send(g, carry):
+        fill(g * GROUP)
+        send_group(g * GROUP - GROUP, 0)
         return carry
 
-    lax.fori_loop(1, DEV, start_send, 0)
-    got_ref[me] = out_ref[me]
+    lax.fori_loop(2, DEV // GROUP, fill_and_send, 0)
+    send_group(DEV - GROUP, 0)
     for copy in fluid_halo:
         copy.wait()
     smooth(fluid_ref, 4, (hy0, hy1, hx0, hx1), field_ref)
@@ -397,17 +432,7 @@
         back(DEV - GROUP + k).start()
     ret_ref[me] = res_ref[me]
 
-    dacc_ref[...] = jnp.zeros_like(dacc_ref)
-
-    def deposit(k, carry):
-        lanes = pl.ds(pl.multiple_of(k * PB, PB), PB)
-        r = row2(rad_ref, k)
-        volume = r * r * r
-        push = -volume * drag_of(seen_ref, mot_ref, r, lanes)
-        deposit_block([volume, push[0:1], push[1:2], push[2:3]], row2(cell_ref, k), dacc_ref)
-        return carry
-
-    lax.fori_loop(0, NBLK, deposit, 0)
+    deposit_four(seen_ref, mot_ref, rad_ref, cell_ref, dacc_ref)
     unfold(dacc_ref, 4, dep_ref)
     edges(dep_ref, 4, gy0, gy1, gx0, gx1)
     dep_halo = halo_copies((gy0, gy1, gx0, gx1), (ky0, ky1, kx0, kx1), ks_sem, kr_sem)
@@ -457,7 +482,7 @@
             VMEM((DEV, 8, 128), F32),
             VMEM((DEV, 128, 128), I32),
             VMEM((1024, 128), F32),
-            VMEM((512, 512), BF16),
+            VMEM((1024, 256), BF16),
             VMEM((2, 512, 128), F32),
             VMEM((1032, 128), F32),
             *halo_scratch(4), *halo_scratch(4), *halo_scratch(4), *halo_scratch(4),
@@ -470,21 +495,21 @@
 
 
 def fetch_kernel(
-    owner_ref, sc_ref, q_ref, cell_ref, ret_ref, seen_ref, mot_ref, rad_ref, tmp_ref,
-    next_ref, dep_ref,
+    owner_ref, sc_ref, q_ref, cell_ref, ret_ref, seen_ref, mot_ref, rad_ref, tmp_ref, spread_ref, fluid_ref,
+    next_ref, dep_ref, fluid_next_ref, void_ref,
     dense_ref, left_ref, acc_ref,
 ):
     lane = iota((8, 128), 1)
 
-    def pack(b, carry):
-        start = sc_ref[0, b]
+    def pack(b, open_tile):
+        start, after = sc_ref[0, b], sc_ref[0, jnp.minimum(b + 1, DEV - 1)]
         tile, off = jnp.clip(start >> 7, 0, 64), start & 127
         mine = pltpu.roll(ret_ref[owner_ref[b]], off, 1)
-        dense_ref[tile] = jnp.where(lane < off, dense_ref[tile], mine)
-        dense_ref[tile + 1] = mine
-        return carry
-
-    lax.fori_loop(0, DEV, pack, 0, unroll=2)
+        merged = jnp.where(lane < off, open_tile, mine)
+        dense_ref[tile] = merged
+        return jnp.where((after >> 7) == (start >> 7), merged, mine)
+
+    lax.fori_loop(0, DEV, pack, jnp.zeros((8, 128), F32), unroll=8)
     hi, lo = split2(dense_ref[0:64].reshape(512, 128))
     left_ref[:, 0:128] = hi
     left_ref[:, 128:256] = lo
@@ -513,54 +538,56 @@
 
     lax.fori_loop(0, NBLK, step, 0)
     unfold(acc_ref, 1, dep_ref)
-
-
-def fetch(owner, sc, q, cell, ret, seen, mot, rad, tmp):
+    crowding = 1.0 + 4.0 * spread_ref[0:256, :]
+    void_ref[...] = 1.0 / crowding
+    scale = 0.4 * crowding
+    for f in range(3):
+        at = slice(256 * f, 256 * f + 256)
+        fluid_next_ref[at, :] = fluid_ref[at, :] + spread_ref[256 * f + 256 : 256 * f + 512, :] * scale
+    fluid_next_ref[768:1024, :] = scale
+
+
+def fetch(owner, sc, q, cell, ret, seen, mot, rad, tmp, spread, fluid):
     return pl.pallas_call(
         fetch_kernel,
-        out_shape=(jax.ShapeDtypeStruct((7, PARTS), F32), jax.ShapeDtypeStruct((264, 128), F32)),
-        in_specs=[pl.BlockSpec(memory_space=pltpu.SMEM)] * 2 + vmem_specs(7),
-        out_specs=tuple(vmem_specs(2)),
+        out_shape=(
+            jax.ShapeDtypeStruct((7, PARTS), F32),
+            jax.ShapeDtypeStruct((264, 128), F32),
+            jax.ShapeDtypeStruct((1024, 128), F32),
+            jax.ShapeDtypeStruct((256, 128), F32),
+        ),
+        in_specs=[pl.BlockSpec(memory_space=pltpu.SMEM)] * 2 + vmem_specs(9),
+        out_specs=tuple(vmem_specs(4)),
         scratch_shapes=[VMEM((66, 8, 128), F32), VMEM((512, 256), BF16), VMEM((2, 128, 128), F32)],
         name="fetch",
-    )(owner, sc, q, cell, ret, seen, mot, rad, tmp)
-
-
-def end_kernel(
-    dep_ref, spread_ref, fluid_ref, next_ref, void_ref,
-    heat_ref, ey0, ey1, ex0, ex1, hy0, hy1, hx0, hx1, hs_sem, hr_sem,
-):
+    )(owner, sc, q, cell, ret, seen, mot, rad, tmp, spread, fluid)
+
+
+def end_kernel(dep_ref, heat_ref, ey0, ey1, ex0, ex1, hy0, hy1, hx0, hx1, hs_sem, hr_sem):
     barrier = pltpu.get_barrier_semaphore()
     for dev in neighbours():
         pl.semaphore_signal(barrier, inc=1, device_id=dev, device_id_type=LOGICAL)
     edges(dep_ref, 1, ey0, ey1, ex0, ex1)
-    crowding = 1.0 + 4.0 * spread_ref[0:256, :]
-    void_ref[...] = 1.0 / crowding
-    scale = 0.4 * crowding
     pl.semaphore_wait(barrier, 4)
     halo = halo_copies((ey0, ey1, ex0, ex1), (hy0, hy1, hx0, hx1), hs_sem, hr_sem)
     for copy in halo:
         copy.start()
-    for f in range(3):
-        at = slice(256 * f, 256 * f + 256)
-        next_ref[at, :] = fluid_ref[at, :] + spread_ref[256 * f + 256 : 256 * f + 512, :] * scale
     for copy in halo:
         copy.wait()
     smooth(dep_ref, 1, (hy0, hy1, hx0, hx1), heat_ref)
-    next_ref[768:1024, :] = fluid_ref[768:1024, :] + heat_ref[...] * scale
-
-
-def end(dep, spread, fluid):
+
+
+def end(dep):
     dma = pltpu.SemaphoreType.DMA
     return pl.pallas_call(
         end_kernel,
-        out_shape=(jax.ShapeDtypeStruct((1024, 128), F32), jax.ShapeDtypeStruct((256, 128), F32)),
-        in_specs=vmem_specs(3),
-        out_specs=tuple(vmem_specs(2)),
-        scratch_shapes=[VMEM((256, 128), F32), *halo_scratch(1), *halo_scratch(1), dma((4,)), dma((4,))],
+        out_shape=jax.ShapeDtypeStruct((256, 128), F32),
+        in_specs=vmem_specs(1),
+        out_specs=pl.BlockSpec(memory_space=VMEM),
+        scratch_shapes=[*halo_scratch(1), *halo_scratch(1), dma((4,)), dma((4,))],
         compiler_params=pltpu.CompilerParams(collective_id=1, has_side_effects=True),
         name="end",
-    )(dep, spread, fluid)
+    )(dep)
 
 
 def shards(fluid, pos, mot, rad, tmp, cell, box, box_owner, mask):
@@ -568,8 +595,10 @@
     cell2, box2 = cell.reshape(64, 128), box.reshape(64, 128)
     fluid2 = fluid.reshape(1024, 128)
     ret, q, sc, seen, spread = main(box_owner.reshape(1, 128), box2, pos, mot, rad2, tmp2, cell2, fluid2, mask)
-    nxt, dep = fetch(box_owner, sc, q, cell2, ret, seen, mot, rad2, tmp2)
-    fluid_next, void = end(dep, spread, fluid2)
+    nxt, dep, fluid_next, void = fetch(box_owner, sc, q, cell2, ret, seen, mot, rad2, tmp2, spread, fluid2)
+    heat = end(dep)
+    last = fluid2[768:1024] + heat * fluid_next[768:1024]
+    fluid_next = lax.dynamic_update_slice(fluid_next, last, (768, 0))
     return fluid_next.reshape(4, 32, 8, 128), void.reshape(32, 8, 128), nxt
 
 

time: 111 us -> 76 us (0.68)
  Pallas kernels: 107 us -> 73.4 us
  local copies, waits for them, and re-layouts: 3.44 us -> 0 us
  other arithmetic: 0 us -> 1.71 us
    pallas_call x1, Pallas kernels: 73.5 us -> 56.1 us  [main(): pl.pallas_call(main_kernel, out_shape=(jax.ShapeDtypeStruct((DEV, 8, 128)...]
    pallas_call x1, Pallas kernels: 23.3 us -> 9 us  [fetch(): pl.pallas_call(fetch_kernel, out_shape=(jax.ShapeDtypeStruct((7, PARTS),...]
    unnamed x2 -> x0, local copies, waits for them, and re-layouts: 3.44 us -> none
    dynamic_update_slice x0 -> x1, other arithmetic: none -> 1.71 us  [shards(): fluid_next = lax.dynamic_update_slice(fluid_next, last, (768, 0))]
    pallas_call x1, Pallas kernels: 9.93 us -> 8.3 us  [end(): pl.pallas_call(end_kernel, out_shape=jax.ShapeDtypeStruct((256, 128), F32...]
where the time goes in v3:
time: 76 us; the launch traced here: 75.8 us
  Pallas kernels  73.4 us (97%)
  other arithmetic  1.71 us (2%)
    pallas_call x1, Pallas kernels, main(): pl.pallas_call(main_kernel, out_shape=(jax.ShapeDtypeStruct((DEV, 8, 128)...  56.1 us
    pallas_call x1, Pallas kernels, fetch(): pl.pallas_call(fetch_kernel, out_shape=(jax.ShapeDtypeStruct((7, PARTS),...  9 us
    pallas_call x1, Pallas kernels, end(): pl.pallas_call(end_kernel, out_shape=jax.ShapeDtypeStruct((256, 128), F32...  8.3 us
    dynamic_update_slice x1, other arithmetic, shards(): fluid_next = lax.dynamic_update_slice(fluid_next, last, (768, 0))  1.71 us

profile of v3, /device:TPU:0, one launch (start us, length us, event | category | flops | bytes accessed | tf_op | source)
XLA Modules:
  0.0 75.8 jit_solution(13050868164430312555)
XLA Ops:
  0.6 56.1 %main.1 = (f32[128,8,128]{2,1,0:T(8,128)}, s32[64,128]{1,0:T(8,128)}, s32[8,128]{1,0:T(8,128)}, f32[4,8192]{1,0:T(4,128)}, f32[1024,128]{1,0:T(8,128)}) custom-call(s32[1,128]{1,0:T(1,128)} %bitcast.22, s32[64,128]{1,0:T(8,128)} %bitcast.20, f32[3,8192]{1,0:T(4,128)} %pos_ref.1, f32[6,8192]{1,0:T(8,128)} %mot_ref.3, f32[64,128]{1,0:T(8,128)} %bitcast.14, ...), custom_call_target="tpu_custom_call" | custom-call | tf_op jit(solution)/shard_map/main/pallas_call | solution.py:464
  56.8 9.0 %fetch.1 = (f32[7,8192]{1,0:T(8,128)}, f32[264,128]{1,0:T(8,128)}, f32[1024,128]{1,0:T(8,128)}, f32[256,128]{1,0:T(8,128)}) custom-call(s32[128]{0:T(128)} %owner_ref.1, s32[8,128]{1,0:T(8,128)} %get-tuple-element.12.sc_ref, s32[64,128]{1,0:T(8,128)} %get-tuple-element.13.q_ref, s32[64,128]{1,0:T(8,128)} %bitcast.19, ...), custom_call_target="tpu_custom_call" | custom-call | tf_op jit(solution)/shard_map/fetch/pallas_call | solution.py:551
  65.7 8.3 %end.1 = f32[256,128]{1,0:T(8,128)} custom-call(f32[264,128]{1,0:T(8,128)} %get-tuple-element.18.dep_ref), custom_call_target="tpu_custom_call" | custom-call | tf_op jit(solution)/shard_map/end/pallas_call | solution.py:582
  74.1 1.7 %fusion = f32[1024,128]{1,0:T(8,128)} fusion(f32[1024,128]{1,0:T(8,128)} %get-tuple-element.17, f32[256,128]{1,0:T(8,128)} %end.1, f32[4,32,8,128]{3,2,1,0:T(8,128)} %param.9), kind=kLoop, calls=%fused_computation.1 | loop fusion | flops 65536 | bytes 524288 | tf_op jit(solution)/shard_map/dynamic_update_slice | solution.py:601

commit v4 on v3

--- a/solution.py
+++ b/solution.py
@@ -70,7 +70,7 @@
         rank_ref[pl.ds(2 * k + 1, 1), :] = rank[:, 128:]
         return before + jnp.sum(jnp.where(match, 1.0, 0.0), axis=1, keepdims=True)
 
-    counts = lax.fori_loop(0, PARTS // RB, rank_step, jnp.zeros((DEV, 1), F32), unroll=8)
+    counts = lax.fori_loop(0, PARTS // RB, rank_step, jnp.zeros((DEV, 1), F32), unroll=True)
     down, over = iota((DEV, DEV), 0), iota((DEV, DEV), 1)
     wide = jnp.broadcast_to(counts, (DEV, DEV))
     start_row = jnp.sum(jnp.where(down < over, wide, 0.0), axis=0, keepdims=True)
@@ -302,7 +302,8 @@
     lax.fori_loop(0, NBLK, step, 0)
 
 
-GROUP = 8
+GROUP = 16
+FILL = 8
 
 
 def main_kernel(
@@ -347,52 +348,45 @@
         peer = lax.rem(me + d, DEV)
         return pltpu.make_async_remote_copy(
             out_ref.at[peer, pl.ds(0, 11)], got_ref.at[me, pl.ds(0, 11)],
-            send_sem.at[d], got_sem.at[me], device_id=peer, device_id_type=LOGICAL,
+            send_sem, got_sem.at[me], device_id=peer, device_id_type=LOGICAL,
         )
 
     def got(d):
         peer = lax.rem(me + DEV - d, DEV)
         return pltpu.make_async_remote_copy(
             out_ref.at[peer, pl.ds(0, 11)], got_ref.at[peer, pl.ds(0, 11)],
-            send_sem.at[d], got_sem.at[peer], device_id=peer, device_id_type=LOGICAL,
+            send_sem, got_sem.at[peer], device_id=peer, device_id_type=LOGICAL,
         )
 
     def back(d):
         peer = lax.rem(me + DEV - d, DEV)
         return pltpu.make_async_remote_copy(
             res_ref.at[peer, pl.ds(0, 7)], ret_ref.at[me, pl.ds(0, 7)],
-            back_sem.at[d], ret_sem.at[me], device_id=peer, device_id_type=LOGICAL,
+            back_sem, ret_sem, device_id=peer, device_id_type=LOGICAL,
         )
 
-    def returned(d):
-        peer = lax.rem(me + d, DEV)
-        return pltpu.make_async_remote_copy(
-            res_ref.at[peer, pl.ds(0, 7)], ret_ref.at[peer, pl.ds(0, 7)],
-            back_sem.at[d], ret_sem.at[peer], device_id=peer, device_id_type=LOGICAL,
-        )
-
     def fill(first):
-        peers = [lax.rem(me + first + k, DEV) for k in range(GROUP)]
+        peers = [lax.rem(me + first + k, DEV) for k in range(FILL)]
         rows = [window(sorted_ref, smem_ref, p) for p in peers]
         for p, r in zip(peers, rows):
             out_ref[p] = r
 
     def send_group(first, skip):
-        for k in range(skip, GROUP):
+        for k in range(skip, FILL):
             send(first + k).start()
 
     fill(0)
     got_ref[me] = out_ref[me]
-    fill(GROUP)
+    fill(FILL)
     send_group(0, 1)
 
     def fill_and_send(g, carry):
-        fill(g * GROUP)
-        send_group(g * GROUP - GROUP, 0)
+        fill(g * FILL)
+        send_group(g * FILL - FILL, 0)
         return carry
 
-    lax.fori_loop(2, DEV // GROUP, fill_and_send, 0)
-    send_group(DEV - GROUP, 0)
+    lax.fori_loop(2, DEV // FILL, fill_and_send, 0)
+    send_group(DEV - FILL, 0)
     for copy in fluid_halo:
         copy.wait()
     smooth(fluid_ref, 4, (hy0, hy1, hx0, hx1), field_ref)
@@ -439,13 +433,15 @@
     for copy in dep_halo:
         copy.start()
 
-    def close(d, carry):
-        send(d).wait_send()
-        back(d).wait_send()
-        returned(d).wait_recv()
-        return carry
-
-    lax.fori_loop(1, DEV, close, 0)
+    others, beside = pl.ds(0, DEV - 1), lax.rem(me + 1, DEV)
+    pltpu.make_async_remote_copy(
+        out_ref.at[others, pl.ds(0, 11)], got_ref.at[others, pl.ds(0, 11)],
+        send_sem, got_sem.at[0], device_id=beside, device_id_type=LOGICAL,
+    ).wait_send()
+    pltpu.make_async_remote_copy(
+        res_ref.at[others, pl.ds(0, 7)], ret_ref.at[others, pl.ds(0, 7)],
+        back_sem, ret_sem, device_id=beside, device_id_type=LOGICAL,
+    ).wait()
     for copy in dep_halo:
         copy.wait()
     smooth(dep_ref, 4, (ky0, ky1, kx0, kx1), spread_ref)
@@ -486,7 +482,7 @@
             VMEM((2, 512, 128), F32),
             VMEM((1032, 128), F32),
             *halo_scratch(4), *halo_scratch(4), *halo_scratch(4), *halo_scratch(4),
-            dma, dma((DEV,)), dma((DEV,)), dma((DEV,)), dma((DEV,)), dma((8,)),
+            dma, dma, dma((DEV,)), dma, dma, dma((8,)),
             dma((4,)), dma((4,)), dma((4,)), dma((4,)),
         ],
         compiler_params=pltpu.CompilerParams(collective_id=0, has_side_effects=True),

time: 76 us -> 69.9 us (0.920)
  Pallas kernels: 73.4 us -> 67.3 us
    pallas_call x1, Pallas kernels: 56.1 us -> 50 us  [main(): pl.pallas_call(main_kernel, out_shape=(jax.ShapeDtypeStruct((DEV, 8, 128)...]
where the time goes in v4:
time: 69.9 us; the launch traced here: 69.7 us
  Pallas kernels  67.3 us (96%)
  other arithmetic  1.71 us (2%)
    pallas_call x1, Pallas kernels, main(): pl.pallas_call(main_kernel, out_shape=(jax.ShapeDtypeStruct((DEV, 8, 128)...  50 us
    pallas_call x1, Pallas kernels, fetch(): pl.pallas_call(fetch_kernel, out_shape=(jax.ShapeDtypeStruct((7, PARTS),...  9 us
    pallas_call x1, Pallas kernels, end(): pl.pallas_call(end_kernel, out_shape=jax.ShapeDtypeStruct((256, 128), F32...  8.3 us
    dynamic_update_slice x1, other arithmetic, shards(): fluid_next = lax.dynamic_update_slice(fluid_next, last, (768, 0))  1.71 us

profile of v4, /device:TPU:0, one launch (start us, length us, event | category | flops | bytes accessed | tf_op | source)
XLA Modules:
  0.0 69.7 jit_solution(11370951404402063308)
XLA Ops:
  0.6 50.0 %main.1 = (f32[128,8,128]{2,1,0:T(8,128)}, s32[64,128]{1,0:T(8,128)}, s32[8,128]{1,0:T(8,128)}, f32[4,8192]{1,0:T(4,128)}, f32[1024,128]{1,0:T(8,128)}) custom-call(s32[1,128]{1,0:T(1,128)} %bitcast.22, s32[64,128]{1,0:T(8,128)} %bitcast.20, f32[3,8192]{1,0:T(4,128)} %pos_ref.1, f32[6,8192]{1,0:T(8,128)} %mot_ref.3, f32[64,128]{1,0:T(8,128)} %bitcast.14, ...), custom_call_target="tpu_custom_call" | custom-call | tf_op jit(solution)/shard_map/main/pallas_call | solution.py:460
  50.6 9.0 %fetch.1 = (f32[7,8192]{1,0:T(8,128)}, f32[264,128]{1,0:T(8,128)}, f32[1024,128]{1,0:T(8,128)}, f32[256,128]{1,0:T(8,128)}) custom-call(s32[128]{0:T(128)} %owner_ref.1, s32[8,128]{1,0:T(8,128)} %get-tuple-element.12.sc_ref, s32[64,128]{1,0:T(8,128)} %get-tuple-element.13.q_ref, s32[64,128]{1,0:T(8,128)} %bitcast.19, ...), custom_call_target="tpu_custom_call" | custom-call | tf_op jit(solution)/shard_map/fetch/pallas_call | solution.py:547
  59.6 8.3 %end.1 = f32[256,128]{1,0:T(8,128)} custom-call(f32[264,128]{1,0:T(8,128)} %get-tuple-element.18.dep_ref), custom_call_target="tpu_custom_call" | custom-call | tf_op jit(solution)/shard_map/end/pallas_call | solution.py:578
  68.0 1.7 %fusion = f32[1024,128]{1,0:T(8,128)} fusion(f32[1024,128]{1,0:T(8,128)} %get-tuple-element.17, f32[256,128]{1,0:T(8,128)} %end.1, f32[4,32,8,128]{3,2,1,0:T(8,128)} %param.9), kind=kLoop, calls=%fused_computation.1 | loop fusion | flops 65536 | bytes 524288 | tf_op jit(solution)/shard_map/dynamic_update_slice | solution.py:597

commit v5 on v4

--- a/solution.py
+++ b/solution.py
@@ -13,7 +13,7 @@
 DEV = 128
 PARTS = 8192
 RB = 256
-PB = 2048
+PB = 4096
 NBLK = PARTS // PB
 LOG2E = 1.4426950408889634
 VMEM = pltpu.VMEM

time: 69.9 us -> 69 us (0.987)
  Pallas kernels: 67.3 us -> 66.4 us
where the time goes in v5:
time: 69 us; the launch traced here: 68.8 us
  Pallas kernels  66.4 us (96%)
  other arithmetic  1.71 us (2%)
    pallas_call x1, Pallas kernels, main(): pl.pallas_call(main_kernel, out_shape=(jax.ShapeDtypeStruct((DEV, 8, 128)...  49.5 us
    pallas_call x1, Pallas kernels, fetch(): pl.pallas_call(fetch_kernel, out_shape=(jax.ShapeDtypeStruct((7, PARTS),...  8.62 us
    pallas_call x1, Pallas kernels, end(): pl.pallas_call(end_kernel, out_shape=jax.ShapeDtypeStruct((256, 128), F32...  8.3 us
    dynamic_update_slice x1, other arithmetic, shards(): fluid_next = lax.dynamic_update_slice(fluid_next, last, (768, 0))  1.71 us

profile of v5, /device:TPU:0, one launch (start us, length us, event | category | flops | bytes accessed | tf_op | source)
XLA Modules:
  0.0 68.8 jit_solution(15387959078806220796)
XLA Ops:
  0.6 49.5 %main.1 = (f32[128,8,128]{2,1,0:T(8,128)}, s32[64,128]{1,0:T(8,128)}, s32[8,128]{1,0:T(8,128)}, f32[4,8192]{1,0:T(4,128)}, f32[1024,128]{1,0:T(8,128)}) custom-call(s32[1,128]{1,0:T(1,128)} %bitcast.22, s32[64,128]{1,0:T(8,128)} %bitcast.20, f32[3,8192]{1,0:T(4,128)} %pos_ref.1, f32[6,8192]{1,0:T(8,128)} %mot_ref.3, f32[64,128]{1,0:T(8,128)} %bitcast.14, ...), custom_call_target="tpu_custom_call" | custom-call | tf_op jit(solution)/shard_map/main/pallas_call | solution.py:460
  50.1 8.6 %fetch.1 = (f32[7,8192]{1,0:T(8,128)}, f32[264,128]{1,0:T(8,128)}, f32[1024,128]{1,0:T(8,128)}, f32[256,128]{1,0:T(8,128)}) custom-call(s32[128]{0:T(128)} %owner_ref.1, s32[8,128]{1,0:T(8,128)} %get-tuple-element.12.sc_ref, s32[64,128]{1,0:T(8,128)} %get-tuple-element.13.q_ref, s32[64,128]{1,0:T(8,128)} %bitcast.19, ...), custom_call_target="tpu_custom_call" | custom-call | tf_op jit(solution)/shard_map/fetch/pallas_call | solution.py:547
  58.7 8.3 %end.1 = f32[256,128]{1,0:T(8,128)} custom-call(f32[264,128]{1,0:T(8,128)} %get-tuple-element.18.dep_ref), custom_call_target="tpu_custom_call" | custom-call | tf_op jit(solution)/shard_map/end/pallas_call | solution.py:578
  67.1 1.7 %fusion = f32[1024,128]{1,0:T(8,128)} fusion(f32[1024,128]{1,0:T(8,128)} %get-tuple-element.17, f32[256,128]{1,0:T(8,128)} %end.1, f32[4,32,8,128]{3,2,1,0:T(8,128)} %param.9), kind=kLoop, calls=%fused_computation.1 | loop fusion | flops 65536 | bytes 524288 | tf_op jit(solution)/shard_map/dynamic_update_slice | solution.py:597
